TPU v7x, 32 devices: a whole 2x2x4 slice. The times are simulated.
32 devices in a mesh: groups: 2 (over y), tm: 4 (over z), space: 2 (over x), mp: 2 (over core).
Axes of the slice: x: 2, y: 2, z: 4, core: 2. Of those that a mesh axis runs over, the one named last changes fastest.
Arguments:
- query_proj: bfloat16 [16, 16, 8, 2240], P(('groups', 'tm'), 'space', None, 'mp'), parts along dimension 0, may hold values from -6 to 6
- key_proj: bfloat16 [16, 16, 8, 2240], P(('groups', 'tm'), 'space', None, 'mp'), parts along dimension 0, may hold values from -6 to 6
- value_proj: bfloat16 [16, 16, 8, 2240], P(('groups', 'tm'), 'space', None, 'mp'), parts along dimension 0, may hold values from -6 to 6
- expanded: bfloat16 [16, 16, 8, 2, 6720], P(('groups', 'tm'), 'space', None, None, 'mp'), parts along dimension 0, may hold values from -6 to 6
- spatial_weight: float32 [3, 3, 2, 6720], P(None, None, None, 'mp'), may hold values from -0.6 to 0.6
- temporal_weight: float32 [3, 2, 6720], P(None, None, 'mp'), may hold values from -1 to 1
Outputs:
- attended: bfloat16 [16, 16, 8, 2240], P(('groups', 'tm'), 'space', None, 'mp'), parts along dimension 0
- gated_hidden: bfloat16 [16, 16, 8, 6720], P(('groups', 'tm'), 'space', None, 'mp'), parts along dimension 0
There are 2 independent parts, one for each index of `groups`. A program takes and returns all parts, laid end to end along the dimension named above; an argument that names none is the same for every part. Nothing has to cross between parts.
All inputs are finite; a program needn't handle non-finite values.
Results may differ from a plain program's by a relative error of at most 0.0059.
Values may be sent and summed in bfloat16 or wider, within the bound.
No kernel may reach another device: no remote copies, remote signals or barrier semaphores. Data moves between devices by JAX's collectives and lax.ppermute only.
A program may use at most 64 MiB of HBM per device.

v0:
```python
import jax
import jax.numpy as jnp
from jax import lax
from jax.sharding import PartitionSpec as P

HEAD_DIM = 32


def carried_in(value, axis, join, neutral):
    count, mine = (lax.axis_size(axis), lax.axis_index(axis))
    pieces = jax.tree.map(lambda part: lax.all_gather(part, axis), value)
    so_far = jax.tree.map(
        lambda part, zero: jnp.full_like(part, 0) + jnp.asarray(zero, part.dtype), value, neutral
    )

    def turn(position, so_far):
        longer = join(so_far, jax.tree.map(lambda part: part[position], pieces))
        return jax.tree.map(lambda new, old: jnp.where(position < mine, new, old), longer, so_far)

    return lax.fori_loop(0, count - 1, turn, so_far)


def padded_2(cells, sides, width):
    for axis, dim in sides:
        count = lax.axis_size(axis)
        ends = count - 1
        head = lax.slice_in_dim(cells, 0, width, axis=dim)
        tail = lax.slice_in_dim(cells, cells.shape[dim] - width, cells.shape[dim], axis=dim)
        cells = jnp.concatenate(
            [
                lax.ppermute(tail, axis, [(i, (i + 1) % count) for i in range(ends)]),
                cells,
                lax.ppermute(head, axis, [((i + 1) % count, i) for i in range(ends)]),
            ],
            axis=dim,
        )
    return cells


def passed_along(value, axis, steps):
    count = lax.axis_size(axis)
    first, last = (max(0, -steps), min(count, count - steps))
    return lax.ppermute(value, axis, [(source, source + steps) for source in range(first, last)])


def add_states(first_pair, second_pair):
    return (first_pair[0] + second_pair[0], first_pair[1] + second_pair[1])


def earlier_states(states):
    empty = (jnp.zeros_like(states[0]), jnp.zeros_like(states[1]))
    return carried_in(states, "tm", add_states, empty)


def conv_block(extended, spatial_weight):
    row_count = extended.shape[1] - 2
    col_count = extended.shape[2]
    padded = jnp.pad(extended, ((0, 0), (0, 0), (1, 1), (0, 0), (0, 0)))
    summed = jnp.zeros((extended.shape[0], row_count, col_count) + extended.shape[3:], jnp.float32)
    for row_tap in range(3):
        for col_tap in range(3):
            summed = (
                summed
                + padded[:, row_tap : row_tap + row_count, col_tap : col_tap + col_count].astype(
                    jnp.float32
                )
                * spatial_weight[row_tap, col_tap]
            )
    return summed.astype(jnp.bfloat16)


def on_device(query_proj, key_proj, value_proj, expanded, spatial_weight, temporal_weight):
    frames = query_proj.shape[0]
    row_count = query_proj.shape[1]
    col_count = query_proj.shape[2]
    channels = query_proj.shape[3]
    head_count = channels // HEAD_DIM
    key_relu = jnp.maximum(key_proj, 0).reshape(-1, head_count, HEAD_DIM)
    value_rows = value_proj.reshape(-1, head_count, HEAD_DIM)
    kv_state = jnp.einsum(
        "thd,the->dhe", key_relu, value_rows, preferred_element_type=jnp.float32
    ).reshape(HEAD_DIM, channels)
    key_sum = jnp.sum(key_relu.astype(jnp.float32), axis=0).reshape(channels)
    local_states = (kv_state, key_sum)
    before = earlier_states(local_states)
    combined = lax.psum(add_states(before, local_states), "space")
    query_relu = jnp.maximum(query_proj, 0).reshape(-1, head_count, HEAD_DIM).astype(jnp.float32)
    numerator = jnp.einsum(
        "thd,dhe->the",
        query_relu,
        combined[0].reshape(HEAD_DIM, head_count, HEAD_DIM),
        precision=lax.Precision.HIGHEST,
    )
    denominator = (
        jnp.einsum(
            "thd,hd->th",
            query_relu,
            combined[1].reshape(head_count, HEAD_DIM),
            precision=lax.Precision.HIGHEST,
        )
        + 1.0
    )
    attended = (
        (numerator / denominator[..., None])
        .reshape(frames, row_count, col_count, channels)
        .astype(jnp.bfloat16)
    )
    extended = padded_2(expanded, (("space", 1),), 1)
    spatial = conv_block(extended, spatial_weight)
    earlier_frames = passed_along(spatial, "tm", 1)
    timeline = jnp.concatenate([earlier_frames, spatial], axis=0)
    mixed = (
        timeline[:-2].astype(jnp.float32) * temporal_weight[0]
        + timeline[1:-1].astype(jnp.float32) * temporal_weight[1]
        + timeline[2:].astype(jnp.float32) * temporal_weight[2]
    )
    gated_hidden = (mixed[..., 0, :] * jax.nn.silu(mixed[..., 1, :])).astype(jnp.bfloat16)
    return (attended, gated_hidden)


def solution(mesh):
    return jax.shard_map(
        on_device,
        mesh=mesh,
        in_specs=(
            P(("groups", "tm"), "space", None, "mp"),
            P(("groups", "tm"), "space", None, "mp"),
            P(("groups", "tm"), "space", None, "mp"),
            P(("groups", "tm"), "space", None, None, "mp"),
            P(None, None, None, "mp"),
            P(None, None, "mp"),
        ),
        out_specs=(
            P(("groups", "tm"), "space", None, "mp"),
            P(("groups", "tm"), "space", None, "mp"),
        ),
        check_vma=False,
    )
```

profile of v0, /device:TPU:0, one launch (start us, length us, event | category | flops | bytes accessed | tf_op | source)
XLA Modules:
  0.0 113.3 jit_solution(13310139821514599711)
XLA Ops:
  7.2 1.7 %copy.39 = bf16[2,8,8,2,3360]{4,2,1,0,3:T(8,128)(2,1)S(1)} copy(bf16[2,8,8,2,3360]{4,3,2,1,0:T(2,128)(2,1)} %param.11) | data formatting | bytes 3440640 | tf_op args[3]
  8.9 0.8 fusion.15
  9.7 5.5 %collective-permute-start = (bf16[2,1,8,2,3360]{4,2,1,0,3:T(8,128)(2,1)}, bf16[2,1,8,2,3360]{4,2,1,0,3:T(8,128)(2,1)}, u32[]{:S(2)}, u32[]{:S(2)}) collective-permute-start(bf16[2,1,8,2,3360]{4,2,1,0,3:T(8,128)(2,1)} %get-tuple-element.149), channel_id=1, source_target_pairs={{0,2},{1,3},{4,6},{5,7},{8,10},{9,11},{12,14},{13,15},{16,18},{17,... | collective-permute-start | bytes 645128 | tf_op jit(solution)/shard_map/ppermute | solution.py:31
  15.3 1.3 %collective-permute-start.1 = (bf16[2,1,8,2,3360]{4,2,1,0,3:T(8,128)(2,1)}, bf16[2,1,8,2,3360]{4,2,1,0,3:T(8,128)(2,1)}, u32[]{:S(2)}, u32[]{:S(2)}) collective-permute-start(bf16[2,1,8,2,3360]{4,2,1,0,3:T(8,128)(2,1)} %get-tuple-element.150), channel_id=1, source_target_pairs={{2,0},{3,1},{6,4},{7,5},{10,8},{11,9},{14,12},{15,13},{18,16},{19,... | collective-permute-start | bytes 645128 | tf_op jit(solution)/shard_map/ppermute | solution.py:33
  16.6 0.1 convert_reduce_fusion
  16.7 1.0 reshape.41
  17.7 2.7 %reshape.42 = bf16[128,35,32]{2,1,0:T(8,128)(2,1)} reshape(bf16[2,8,8,1120]{3,2,1,0:T(8,128)(2,1)} %param.10) | data formatting | bytes 573440 | tf_op jit(solution)/shard_map/reshape | solution.py:79
  20.4 1.8 %convolution_bitcast_fusion.1 = f32[32,35,32]{2,0,1:T(8,128)S(1)} fusion(bf16[128,35,32]{2,1,0:T(8,128)(2,1)} %reshape.42, bf16[128,35,32]{2,1,0:T(8,128)(2,1)S(1)} %reshape.41), kind=kOutput, calls=%fused_computation.21 | convolution fusion | flops 9175040 | bytes 716800 | tf_op jit(solution)/shard_map/thd,the->dhe/dot_general | solution.py:80
  22.2 0.3 copy.34
  22.6 0.2 all_gather_reshape.6
  22.7 0.2 reshape.43
  22.9 0.6 dynamic-slice
  24.2 0.3 dynamic-update-slice
  24.5 19.1 %all-reduce.1 = f32[4480]{0:T(1024)S(1)} all-reduce(f32[4480]{0:T(1024)S(1)} %dynamic-update-slice), channel_id=2, replica_groups=mesh['groups'=2,'tm'=4,'space'=2,'mp'=2] {'tm'}, use_global_device_ids=true, to_apply=%add.1 | all-reduce | flops 4480 | bytes 35840
  43.6 0.1 reshape.47
  43.7 15.5 %all_gather.6 = f32[4,32,1120]{2,1,0:T(8,128)S(1)} all-gather(f32[1,32,1120]{2,1,0:T(8,128)S(1)} %all_gather_reshape.6), channel_id=1, replica_groups=mesh['groups'=2,'tm'=4,'space'=2,'mp'=2] {'tm'}, dimensions={0}, use_global_device_ids=true | all-gather | bytes 716800 | tf_op jit(solution)/shard_map/all_gather | solution.py:11
  59.2 0.3 while.16
  59.6 1.0 copy.36
  60.7 2.7 %fusion.5 = bf16[2,10,10,2,3360]{4,2,1,0,3:T(8,128)(2,1)S(1)} fusion(bf16[2,1,8,2,3360]{4,2,1,0,3:T(8,128)(2,1)} %collective-permute-done.1, bf16[2,8,8,2,3360]{4,2,1,0,3:T(8,128)(2,1)S(1)} %copy.39, bf16[2,1,8,2,3360]{4,2,1,0,3:T(8,128)(2,1)} %collective-permute-done), kind=kLoop, calls=%fused_computation.10 | loop fusion | flops 16128000 | bytes 4838400 | tf_op jit(solution)/shard_map/concatenate | solution.py:29
  63.5 5.1 %add_convert_fusion = bf16[2,8,8,2,3360]{4,2,1,0,3:T(8,128)(2,1)S(1)} fusion(bf16[2,8,8,2,3360]{4,2,1,0,3:T(8,128)(2,1)S(1)} %copy.39, bf16[2,10,10,2,3360]{4,2,1,0,3:T(8,128)(2,1)S(1)} %fusion.5, bf16[2,1,8,2,3360]{4,2,1,0,3:T(8,128)(2,1)} %collective-permute-done.1, bf16[2,1,8,2,3360]{4,2,1,0,3:T(8,128)(2,1)} %collective-permute-done, ...), kind=kLoop, calls=%fused_computation.12 | loop fusion | flops 24944640 | bytes 14434560 | tf_op jit(solution)/shard_map/convert_element_type | solution.py:69
  68.6 2.7 %collective-permute-start.2 = (bf16[2,8,8,2,3360]{4,2,1,0,3:T(8,128)(2,1)S(1)}, bf16[2,8,8,2,3360]{4,2,1,0,3:T(8,128)(2,1)}, u32[]{:S(2)}, u32[]{:S(2)}) collective-permute-start(bf16[2,8,8,2,3360]{4,2,1,0,3:T(8,128)(2,1)S(1)} %add_convert_fusion), channel_id=1, source_target_pairs={{0,4},{4,8},{8,12},{1,5},{5,9},{9,13},{2,6},{6,10},{10,14},{3,7},{... | collective-permute-start | bytes 5160968 | tf_op jit(solution)/shard_map/ppermute | solution.py:43
  71.3 1.0 reshape.45
  72.3 1.5 %copy.37 = bf16[128,35,32]{0,2,1:T(8,128)(2,1)S(1)} copy(bf16[128,35,32]{2,1,0:T(8,128)(2,1)S(1)} %reshape.45) | data formatting | bytes 573440 | tf_op jit(solution)/shard_map/reshape | solution.py:87
  73.8 10.5 %psum.15 = f32[35,32]{1,0:T(8,128)S(1)} all-reduce(f32[35,32]{1,0:T(8,128)S(1)} %reshape.46), channel_id=1, replica_groups=mesh['groups'=2,'tm'=4,'space'=2,'mp'=2] {'space'}, use_global_device_ids=true, to_apply=%region_4.5 | all-reduce | flops 1120 | bytes 8960 | tf_op jit(solution)/shard_map/psum | solution.py:86
  84.3 0.3 fusion.13
  84.7 6.7 %all-reduce.4.cloned.1.call-done = f32[32,35,32]{0,2,1:T(8,128)} async-done(((f32[32,35,32]{0,2,1:T(8,128)}), f32[32,35,32]{0,2,1:T(8,128)}) %all-reduce.4.cloned.1.call-update) | async-done | bytes 143376 | tf_op jit(solution)/shard_map/psum | solution.py:86
  91.5 2.2 %fusion.9 = bf16[128,35,32]{0,2,1:T(8,128)(2,1)} fusion(f32[32,35,32]{0,2,1:T(8,128)} %all-reduce.4.cloned.1.call-done, bf16[128,35,32]{0,2,1:T(8,128)(2,1)S(1)} %copy.37, f32[128,35]{0,1:T(8,128)S(1)} %fusion.12), kind=kOutput, calls=%fused_computation.23 | convolution fusion | flops 55336960 | bytes 734720 | tf_op jit(solution)/shard_map/thd,dhe->the/dot_general | solution.py:88
  93.6 1.9 %copy.38 = bf16[128,35,32]{2,1,0:T(8,128)(2,1)S(1)} copy(bf16[128,35,32]{0,2,1:T(8,128)(2,1)} %fusion.9) | data formatting | bytes 573440 | tf_op jit(solution)/shard_map/convert_element_type | solution.py:106
  95.5 1.4 %convert_element_type.57 = bf16[2,8,8,1120]{3,2,1,0:T(8,128)(2,1)} reshape(bf16[128,35,32]{2,1,0:T(8,128)(2,1)S(1)} %copy.38) | data formatting | bytes 573440 | tf_op jit(solution)/shard_map/convert_element_type | solution.py:106
  96.9 5.5 %collective-permute-done.2 = bf16[2,8,8,2,3360]{4,2,1,0,3:T(8,128)(2,1)} collective-permute-done((bf16[2,8,8,2,3360]{4,2,1,0,3:T(8,128)(2,1)S(1)}, bf16[2,8,8,2,3360]{4,2,1,0,3:T(8,128)(2,1)}, u32[]{:S(2)}, u32[]{:S(2)}) %collective-permute-start.2) | collective-permute-done | bytes 1720352 | tf_op jit(solution)/shard_map/ppermute | solution.py:43
  102.4 2.6 %multiply_add_fusion = f32[2,8,8,2,3360]{4,2,1,0,3:T(8,128)S(1)} fusion(bf16[2,8,8,2,3360]{4,2,1,0,3:T(8,128)(2,1)S(1)} %add_convert_fusion, bf16[2,8,8,2,3360]{4,2,1,0,3:T(8,128)(2,1)} %collective-permute-done.2, f32[2,3360]{1,0:T(2,128)S(1)} %get-tuple-element.161, f32[2,3360]{1,0:T(2,128)S(1)} %get-tuple-element.162, f32[2,3360]{1,0:T(2,128)S(1)} %get-tuple-element.160), kind=kLoop, calls=%fused_computation.11 | loop fusion | flops 7741440 | bytes 6961920 | tf_op jit(solution)/shard_map/add | solution.py:113
  105.1 1.4 %fusion.7 = bf16[2,8,8,3360]{3,2,1,0:T(8,128)(2,1)} fusion(f32[2,8,8,2,3360]{4,2,1,0,3:T(8,128)S(1)} %multiply_add_fusion), kind=kLoop, calls=%fused_computation.16 | loop fusion | flops 2580480 | bytes 4300800 | tf_op jit(solution)/shard_map/convert_element_type | solution.py:117
  (34 shorter events, 0.5 us)
Async XLA Ops:
  7.2 9.4 %copy-start = (bf16[2,8,8,1120]{3,2,1,0:T(8,128)(2,1)S(1)}, bf16[2,8,8,1120]{3,2,1,0:T(8,128)(2,1)}, u32[]{:S(2)}) copy-start(bf16[2,8,8,1120]{3,2,1,0:T(8,128)(2,1)} %param.9) | copy-start | bytes 860164
  7.2 84.3 %all-reduce.4.cloned.1.call-start = ((), (), s32[]{:S(2)}) async-start(), calls=%async_computation | async-start | bytes 1146880 | tf_op jit(solution)/shard_map/psum | solution.py:86
  9.7 51.0 %collective-permute-start = (bf16[2,1,8,2,3360]{4,2,1,0,3:T(8,128)(2,1)}, bf16[2,1,8,2,3360]{4,2,1,0,3:T(8,128)(2,1)}, u32[]{:S(2)}, u32[]{:S(2)}) collective-permute-start(bf16[2,1,8,2,3360]{4,2,1,0,3:T(8,128)(2,1)} %get-tuple-element.149), channel_id=1, source_target_pairs={{0,2},{1,3},{4,6},{5,7},{8,10},{9,11},{12,14},{13,15},{16,18},{17,... | collective-permute-start | bytes 645128 | tf_op jit(solution)/shard_map/ppermute | solution.py:31
  15.3 45.4 %collective-permute-start.1 = (bf16[2,1,8,2,3360]{4,2,1,0,3:T(8,128)(2,1)}, bf16[2,1,8,2,3360]{4,2,1,0,3:T(8,128)(2,1)}, u32[]{:S(2)}, u32[]{:S(2)}) collective-permute-start(bf16[2,1,8,2,3360]{4,2,1,0,3:T(8,128)(2,1)} %get-tuple-element.150), channel_id=1, source_target_pairs={{2,0},{3,1},{6,4},{7,5},{10,8},{11,9},{14,12},{15,13},{18,16},{19,... | collective-permute-start | bytes 645128 | tf_op jit(solution)/shard_map/ppermute | solution.py:33
  17.7 5.3 %copy-start.4 = (u32[32]{0:T(128)S(1)}, u32[32]{0:T(128)}, u32[]{:S(2)}) copy-start(u32[32]{0:T(128)} %constant.48) | copy-start | bytes 388
  22.5 38.1 %copy-start.2 = (f32[3,3,2,3360]{3,2,1,0:T(2,128)S(1)}, f32[3,3,2,3360]{3,2,1,0:T(2,128)}, u32[]{:S(2)}) copy-start(f32[3,3,2,3360]{3,2,1,0:T(2,128)} %param.12) | copy-start | bytes 725764
  63.4 7.8 %copy-start.1 = (bf16[2,8,8,1120]{3,2,1,0:T(8,128)(2,1)S(1)}, bf16[2,8,8,1120]{3,2,1,0:T(8,128)(2,1)}, u32[]{:S(2)}) copy-start(bf16[2,8,8,1120]{3,2,1,0:T(8,128)(2,1)} %param.8) | copy-start | bytes 860164
  68.6 16.1 %copy-start.3 = (f32[3,2,3360]{2,1,0:T(2,128)S(1)}, f32[3,2,3360]{2,1,0:T(2,128)}, u32[]{:S(2)}) copy-start(f32[3,2,3360]{2,1,0:T(2,128)} %param.13) | copy-start | bytes 241924
  68.6 33.9 %collective-permute-start.2 = (bf16[2,8,8,2,3360]{4,2,1,0,3:T(8,128)(2,1)S(1)}, bf16[2,8,8,2,3360]{4,2,1,0,3:T(8,128)(2,1)}, u32[]{:S(2)}, u32[]{:S(2)}) collective-permute-start(bf16[2,8,8,2,3360]{4,2,1,0,3:T(8,128)(2,1)S(1)} %add_convert_fusion), channel_id=1, source_target_pairs={{0,4},{4,8},{8,12},{1,5},{5,9},{9,13},{2,6},{6,10},{10,14},{3,7},{... | collective-permute-start | bytes 5160968 | tf_op jit(solution)/shard_map/ppermute | solution.py:43
Sparse Core Ops, SparseCore 0:
  60.7 30.6 all-reduce.3
where the time goes:
time: 115 us; the launch traced here: 113 us
  blocking collectives  45.2 us (39%)
  local copies, waits for them, and re-layouts  14.9 us (13%)
  between operations  14.9 us (13%)
  waiting for transfers between devices  12.3 us (11%)
  other arithmetic  12.2 us (11%)
  starting transfers between devices  9.53 us (8%)
  matrix products  4.28 us (4%)
    unnamed x1, blocking collectives  19.1 us
    all_gather x1, blocking collectives, carried_in(): pieces = jax.tree.map(lambda part: lax.all_gather(part, axis), value)  15.5 us
    psum x1, blocking collectives, on_device(): combined = lax.psum(add_states(before, local_states), 'space')  10.5 us
    psum x1, waiting for transfers between devices, on_device(): combined = lax.psum(add_states(before, local_states), 'space')  6.73 us
    ppermute x1, starting transfers between devices, padded_2(): lax.ppermute(tail, axis, [(i, (i + 1) % count) for i in range(ends)])  5.55 us
    ppermute x1, waiting for transfers between devices, passed_along(): lax.ppermute(value, axis, [(source, source + steps) for source in range(f...  5.51 us
    convert_element_type x1, other arithmetic, conv_block(): return summed.astype(jnp.bfloat16)  5.09 us
    convert_element_type x2, local copies, waits for them, and re-layouts, on_device(): attended = (numerator / denominator[..., None]).reshape(frames, row_count...  3.31 us
  transfers between devices with their start and end apart: 4, of which 2 were waited for; matrix products, arithmetic and copies ran while one was open for 22% of the time, Pallas kernels for 0%

commit v1 on v0

v1 whole, which is shorter than its diff:
```python
import functools

import jax
import jax.numpy as jnp
from jax import lax
from jax.experimental import pallas as pl
from jax.experimental.pallas import tpu as pltpu
from jax.sharding import PartitionSpec as P

HEAD_DIM = 32
LANES = 128
STATE_ROWS = HEAD_DIM + 8
F32 = jnp.float32
BF16 = jnp.bfloat16


def shifted(value, axis, steps):
    count = lax.axis_size(axis)
    first, last = (max(0, -steps), min(count, count - steps))
    return lax.ppermute(value, axis, [(source, source + steps) for source in range(first, last)])


def rotated(value, axis, steps):
    count = lax.axis_size(axis)
    return lax.ppermute(value, axis, [(source, (source + steps) % count) for source in range(count)])


def edge_rows(frame):
    count, mine = (lax.axis_size("space"), lax.axis_index("space"))
    head, tail = (frame[:, 0], frame[:, -1])
    if count == 2:
        other = lax.ppermute(jnp.where(mine == 0, tail, head), "space", [(0, 1), (1, 0)])
        return (other, other)
    return (shifted(tail, "space", 1), shifted(head, "space", -1))


def params(vmem_mib=16):
    return pltpu.CompilerParams(vmem_limit_bytes=vmem_mib << 20)


VMEM = pl.BlockSpec(memory_space=pltpu.VMEM)
SMEM = pl.BlockSpec(memory_space=pltpu.SMEM)


def lane_tiles(channels, body):
    full = channels // LANES

    @pl.loop(0, full)
    def _(tile):
        body(pl.ds(pl.multiple_of(tile * LANES, LANES), LANES), LANES)

    if channels % LANES:
        body(pl.ds(full * LANES, channels % LANES), channels % LANES)


def tap_weights(weight_ref, part, lanes, width, columns):
    column = lax.broadcasted_iota(jnp.int32, (columns, width), 0)
    taps = []
    for row_tap in range(3):
        row = []
        for col_tap in range(3):
            w = jnp.broadcast_to(weight_ref[row_tap, col_tap, part : part + 1, lanes], (columns, width))
            if col_tap == 0:
                w = jnp.where(column == columns - 1, 0.0, w)
            if col_tap == 2:
                w = jnp.where(column == 0, 0.0, w)
            row.append(w)
        taps.append(row)
    return taps


def conv_rows(rows, taps, columns):
    out = []
    for r in range(len(rows) - 2):
        column_sums = [
            taps[0][b] * rows[r] + taps[1][b] * rows[r + 1] + taps[2][b] * rows[r + 2] for b in range(3)
        ]
        total = (
            column_sums[1]
            + pltpu.roll(column_sums[0], 1, 0)
            + pltpu.roll(column_sums[2], columns - 1, 0)
        )
        out.append(total.astype(BF16))
    return out


def padded_rows(frame_ref, top, bottom, part, lanes):
    row_count = frame_ref.shape[1]
    return (
        [top]
        + [frame_ref[part, r, :, lanes].astype(F32) for r in range(row_count)]
        + [bottom]
    )


def masked(edge_ref, part, lanes, flag):
    return edge_ref[part, :, lanes].astype(F32) * flag


def own_conv_kernel(flags, f0, f1, top0, top1, bot0, bot1, weight, s0, s1):
    columns = f0.shape[2]
    has_top, has_bottom = (flags[0].astype(F32), flags[1].astype(F32))

    def tile(lanes, width):
        for part in range(2):
            taps = tap_weights(weight, part, lanes, width, columns)
            for frame, top, bottom, out in ((f0, top0, bot0, s0), (f1, top1, bot1, s1)):
                rows = padded_rows(
                    frame,
                    masked(top, part, lanes, has_top),
                    masked(bottom, part, lanes, has_bottom),
                    part,
                    lanes,
                )
                for r, value in enumerate(conv_rows(rows, taps, columns)):
                    out[part, r, :, lanes] = value

    lane_tiles(f0.shape[3], tile)


def gate(value, key):
    return value * (key / (1.0 + jnp.exp(-key)))


def mix_kernel(taps_of, flags, raw, top, bottom, near0, near1, weight, temporal, out):
    columns = raw.shape[2]
    has_top, has_bottom = (flags[0].astype(F32), flags[1].astype(F32))

    def tile(lanes, width):
        mixed = []
        for part in range(2):
            taps = tap_weights(weight, part, lanes, width, columns)
            rows = padded_rows(
                raw,
                masked(top, part, lanes, has_top),
                masked(bottom, part, lanes, has_bottom),
                part,
                lanes,
            )
            w = [
                jnp.broadcast_to(temporal[tap, part : part + 1, lanes], (columns, width)) for tap in taps_of
            ]
            mixed.append(
                [
                    w[0] * value.astype(F32)
                    + w[1] * near0[part, r, :, lanes].astype(F32)
                    + w[2] * near1[part, r, :, lanes].astype(F32)
                    for r, value in enumerate(conv_rows(rows, taps, columns))
                ]
            )
        for r in range(raw.shape[1]):
            out[r, :, lanes] = gate(mixed[0][r], mixed[1][r]).astype(BF16)

    lane_tiles(raw.shape[3], tile)


def first_kernel(s0, temporal, out):
    columns = s0.shape[2]

    def tile(lanes, width):
        w = [jnp.broadcast_to(temporal[2, part : part + 1, lanes], (columns, width)) for part in range(2)]
        for r in range(s0.shape[1]):
            mixed = [w[part] * s0[part, r, :, lanes].astype(F32) for part in range(2)]
            out[r, :, lanes] = gate(mixed[0], mixed[1]).astype(BF16)

    lane_tiles(s0.shape[3], tile)


def own_conv(flags, f0, f1, edges0, edges1, weight):
    return pl.pallas_call(
        own_conv_kernel,
        out_shape=(jax.ShapeDtypeStruct(f0.shape, BF16),) * 2,
        in_specs=[SMEM] + [VMEM] * 7,
        out_specs=(VMEM, VMEM),
        compiler_params=params(),
        name="own_conv",
    )(flags, f0, f1, edges0[0], edges1[0], edges0[1], edges1[1], weight)


def mix(taps_of, flags, raw, edges, near0, near1, weight, temporal, name):
    return pl.pallas_call(
        functools.partial(mix_kernel, taps_of),
        out_shape=jax.ShapeDtypeStruct(raw.shape[1:], BF16),
        in_specs=[SMEM] + [VMEM] * 7,
        out_specs=VMEM,
        compiler_params=params(),
        name=name,
    )(flags, raw, edges[0], edges[1], near0, near1, weight, temporal)


def first_frame(s0, temporal):
    return pl.pallas_call(
        first_kernel,
        out_shape=jax.ShapeDtypeStruct(s0.shape[1:], BF16),
        in_specs=[VMEM] * 2,
        out_specs=VMEM,
        compiler_params=params(),
        name="first_frame",
    )(s0, temporal)


def head_mask(width):
    row = lax.broadcasted_iota(jnp.int32, (width, width), 0) // HEAD_DIM
    column = lax.broadcasted_iota(jnp.int32, (width, width), 1) // HEAD_DIM
    return row == column


def lane_groups(channels):
    return [(at, min(LANES, channels - at)) for at in range(0, channels, LANES)]


def state_kernel(key, value, state):
    tokens, channels = key.shape
    chunk = state.shape[2]
    ones = jnp.ones((8, tokens), BF16)
    state[...] = jnp.zeros_like(state)
    for at, width in lane_groups(channels):
        keys = jnp.maximum(key[:, at : at + width], 0)
        product = lax.dot_general(
            keys, value[:, at : at + width], (((0,), (0,)), ((), ())), preferred_element_type=F32
        )
        product = jnp.where(head_mask(width), product, 0.0)
        folded = sum(product[d : d + HEAD_DIM] for d in range(0, width, HEAD_DIM))
        lanes = slice(at % chunk, at % chunk + width)
        state[at // chunk, :HEAD_DIM, lanes] = folded
        state[at // chunk, HEAD_DIM:, lanes] = jnp.dot(ones, keys, preferred_element_type=F32)


def split(value):
    high = value.astype(BF16)
    return (high, (value - high.astype(F32)).astype(BF16))


def attend_kernel(query, state, out):
    channels = query.shape[1]
    chunk = state.shape[2]
    for at, width in lane_groups(channels):
        rows = jnp.maximum(query[:, at : at + width], 0)
        lanes = slice(at % chunk, at % chunk + width)
        mask = head_mask(width)
        folded = state[at // chunk, :HEAD_DIM, lanes]
        kv = jnp.where(mask, jnp.concatenate([folded] * (width // HEAD_DIM), axis=0), 0.0)
        sums = jnp.where(
            mask, jnp.broadcast_to(state[at // chunk, HEAD_DIM : HEAD_DIM + 1, lanes], (width, width)), 0.0
        )
        numerator = sum(jnp.dot(rows, part, preferred_element_type=F32) for part in split(kv))
        denominator = sum(
            lax.dot_general(rows, part, (((1,), (1,)), ((), ())), preferred_element_type=F32)
            for part in split(sums)
        )
        out[:, at : at + width] = (numerator / (denominator + 1.0)).astype(BF16)


def local_state(key, value, chunks):
    channels = key.shape[1]
    groups = pl.cdiv(pl.cdiv(channels, LANES), chunks)
    return pl.pallas_call(
        state_kernel,
        out_shape=jax.ShapeDtypeStruct((chunks, STATE_ROWS, groups * LANES), F32),
        in_specs=[VMEM] * 2,
        out_specs=VMEM,
        compiler_params=params(),
        name="local_state",
    )(key, value)


def attend(query, state):
    return pl.pallas_call(
        attend_kernel,
        out_shape=jax.ShapeDtypeStruct(query.shape, BF16),
        in_specs=[VMEM] * 2,
        out_specs=VMEM,
        compiler_params=params(),
        name="attend",
    )(query, state)


def prefixed_state(state):
    count, mine = (lax.axis_size("space"), lax.axis_index("space"))
    own = lax.dynamic_index_in_dim(state, mine, 0, keepdims=False)
    for step in range(1, count):
        chunk = lax.dynamic_index_in_dim(state, (mine + step) % count, 0, keepdims=False)
        own = own + rotated(chunk, "space", step)
    step = 1
    while step < lax.axis_size("tm"):
        own = own + shifted(own.astype(BF16), "tm", step).astype(F32)
        step *= 2
    whole = lax.dynamic_update_index_in_dim(state, own, mine, 0)
    for step in range(1, count):
        whole = lax.dynamic_update_index_in_dim(
            whole, rotated(own, "space", step), (mine - step) % count, 0
        )
    return whole


def on_device(query_proj, key_proj, value_proj, expanded, spatial_weight, temporal_weight):
    frames, row_count, col_count, channels = query_proj.shape
    assert frames == 2
    space, spaces = (lax.axis_index("space"), lax.axis_size("space"))
    flags = jnp.stack([space > 0, space < spaces - 1]).astype(jnp.int32)

    f0, f1 = (jnp.transpose(expanded[t], (2, 0, 1, 3)) for t in range(2))
    before = shifted(f1, "tm", 1)
    after = shifted(f0, "tm", -1)
    both = edge_rows(jnp.concatenate([f0, f1], axis=0))
    edges0, edges1 = ([edge[2 * t : 2 * t + 2] for edge in both] for t in range(2))

    def tokens(array):
        return array.reshape(-1, channels)

    state = local_state(tokens(key_proj), tokens(value_proj), spaces)
    whole = prefixed_state(state)
    attended = attend(tokens(query_proj), whole).reshape(query_proj.shape)

    s0, s1 = own_conv(flags, f0, f1, edges0, edges1, spatial_weight)
    theirs = mix(
        (2, 0, 1), flags, after, edge_rows(after), s0, s1, spatial_weight, temporal_weight, "mix_after"
    )
    out1 = mix(
        (0, 1, 2), flags, before, edge_rows(before), s0, s1, spatial_weight, temporal_weight, "mix_before"
    )
    out0 = shifted(theirs, "tm", 1)
    out0 = jnp.where(lax.axis_index("tm") == 0, first_frame(s0, temporal_weight), out0)
    return (attended, jnp.stack([out0, out1]))


def solution(mesh):
    return jax.shard_map(
        on_device,
        mesh=mesh,
        in_specs=(
            P(("groups", "tm"), "space", None, "mp"),
            P(("groups", "tm"), "space", None, "mp"),
            P(("groups", "tm"), "space", None, "mp"),
            P(("groups", "tm"), "space", None, None, "mp"),
            P(None, None, None, "mp"),
            P(None, None, "mp"),
        ),
        out_specs=(
            P(("groups", "tm"), "space", None, "mp"),
            P(("groups", "tm"), "space", None, "mp"),
        ),
        check_vma=False,
    )
```

time: 115 us -> 67.4 us (0.59); the launches traced: 113 us -> 66.9 us
  blocking collectives: 45.2 us -> 0 us
  starting transfers between devices: 9.53 us -> 26.7 us
  between operations: 14.9 us -> 0.84 us
  Pallas kernels: 0 us -> 12.1 us
  other arithmetic: 12.2 us -> 4.24 us
  local copies, waits for them, and re-layouts: 14.9 us -> 9.55 us
  matrix products: 4.28 us -> 0 us
    unnamed x1 -> x0, blocking collectives: 19.1 us -> none
    ppermute x3 -> x10, starting transfers between devices: 9.49 us -> 26.7 us  [the longest x5 20.8 us: shifted(): lax.ppermute(value, axis, [(source, source + steps) for source in range(f...]
    all_gather x1 -> x0, blocking collectives: 15.5 us -> none  [carried_in(): pieces = jax.tree.map(lambda part: lax.all_gather(part, axis), value)]
    pallas_call x0 -> x6, Pallas kernels: none -> 12.1 us  [the longest x2 6.43 us: mix(): pl.pallas_call(functools.partial(mix_kernel, taps_of), out_shape=jax.Shap...]
    psum x1 -> x0, blocking collectives: 10.5 us -> none  [on_device(): combined = lax.psum(add_states(before, local_states), 'space')]
    ppermute x3 -> x10, waiting for transfers between devices: 5.52 us -> 13.4 us  [the longest x5 10.8 us: shifted(): lax.ppermute(value, axis, [(source, source + steps) for source in range(f...]
    psum x1 -> x0, waiting for transfers between devices: 6.73 us -> none  [on_device(): combined = lax.psum(add_states(before, local_states), 'space')]
    convert_element_type x2 -> x3, other arithmetic: 6.5 us -> 0.11 us  [the longest x1 0.08 us: on_device(): flags = jnp.stack([space > 0, space < spaces - 1]).astype(jnp.int32)]
  transfers between devices with their start and end apart: 4 -> 10, of which waited for: 2 -> 4; matrix products, arithmetic and copies ran while one was open for 22% -> 14% of each run, Pallas kernels for 0% -> 18%
where the time goes in v1:
time: 67.4 us; the launch traced here: 66.9 us
  starting transfers between devices  26.7 us (40%)
  waiting for transfers between devices  13.4 us (20%)
  Pallas kernels  12.1 us (18%)
  local copies, waits for them, and re-layouts  9.55 us (14%)
  other arithmetic  4.24 us (6%)
  between operations  0.84 us (1%)
    ppermute x5, starting transfers between devices, shifted(): lax.ppermute(value, axis, [(source, source + steps) for source in range(f...  20.8 us
    ppermute x5, waiting for transfers between devices, shifted(): lax.ppermute(value, axis, [(source, source + steps) for source in range(f...  10.8 us
    pallas_call x2, Pallas kernels, mix(): pl.pallas_call(functools.partial(mix_kernel, taps_of), out_shape=jax.Shap...  6.43 us
    ppermute x2, starting transfers between devices, rotated(): lax.ppermute(value, axis, [(source, (source + steps) % count) for source...  3.55 us
    pallas_call x1, Pallas kernels, own_conv(): pl.pallas_call(own_conv_kernel, out_shape=(jax.ShapeDtypeStruct(f0.shape,...  3.29 us
    select_n x3, other arithmetic, edge_rows(): jnp.where(mine == 0, tail, head)  3.04 us
    slice x1, local copies, waits for them, and re-layouts, on_device(): f0, f1 = (jnp.transpose(expanded[t], (2, 0, 1, 3)) for t in range(2))  2.65 us
    ppermute x2, local copies, waits for them, and re-layouts, shifted(): lax.ppermute(value, axis, [(source, source + steps) for source in range(f...  2.46 us
  transfers between devices with their start and end apart: 10, of which 4 were waited for; matrix products, arithmetic and copies ran while one was open for 14% of the time, Pallas kernels for 18%

profile of v1, /device:TPU:0, one launch (start us, length us, event | category | flops | bytes accessed | tf_op | source)
XLA Modules:
  0.0 66.9 jit_solution(18018182159067772052)
XLA Ops:
  0.6 2.6 %fusion.6 = (bf16[1,8,8,2,3360]{4,3,2,1,0:T(2,128)(2,1)S(1)}, bf16[1,8,8,2,3360]{4,3,2,1,0:T(2,128)(2,1)S(1)}) fusion(bf16[2,8,8,2,3360]{4,3,2,1,0:T(2,128)(2,1)} %param.9), kind=kLoop, calls=%fused_computation.22 | loop fusion | bytes 3440640 | tf_op jit(solution)/shard_map/slice | solution.py:302
  3.3 1.0 %copy.23 = bf16[1,8,8,2,3360]{4,2,3,1,0:T(8,128)(2,1)} copy(bf16[1,8,8,2,3360]{4,3,2,1,0:T(2,128)(2,1)S(1)} %get-tuple-element.10) | data formatting | bytes 1720320
  4.3 1.3 %collective-permute-start.5 = (bf16[2,8,8,3360]{3,2,0,1:T(8,128)(2,1)}, bf16[2,8,8,3360]{3,2,0,1:T(8,128)(2,1)}, u32[]{:S(2)}, u32[]{:S(2)}) collective-permute-start(bf16[2,8,8,3360]{3,2,0,1:T(8,128)(2,1)} %bitcast.37), channel_id=1, source_target_pairs={{4,0},{8,4},{12,8},{5,1},{9,5},{13,9},{6,2},{10,6},{14,10},{7,3},{... | collective-permute-start | bytes 2580488 | tf_op jit(solution)/shard_map/ppermute | solution.py:20
  5.6 1.0 %copy.22 = bf16[1,8,8,2,3360]{4,2,3,1,0:T(8,128)(2,1)} copy(bf16[1,8,8,2,3360]{4,3,2,1,0:T(2,128)(2,1)S(1)} %get-tuple-element.11) | data formatting | bytes 1720320
  6.6 6.5 %collective-permute-start.8 = (bf16[2,8,8,3360]{3,2,0,1:T(8,128)(2,1)}, bf16[2,8,8,3360]{3,2,0,1:T(8,128)(2,1)}, u32[]{:S(2)}, u32[]{:S(2)}) collective-permute-start(bf16[2,8,8,3360]{3,2,0,1:T(8,128)(2,1)} %bitcast.36), channel_id=1, source_target_pairs={{0,4},{4,8},{8,12},{1,5},{5,9},{9,13},{2,6},{6,10},{10,14},{3,7},{... | collective-permute-start | bytes 2580488 | tf_op jit(solution)/shard_map/ppermute | solution.py:20
  13.1 0.3 local_state.1
  13.5 2.0 %collective-permute-start = (f32[40,640]{1,0:T(8,128)S(1)}, f32[40,640]{1,0:T(8,128)S(1)}, u32[]{:S(2)}, u32[]{:S(2)}) collective-permute-start(f32[40,640]{1,0:T(8,128)S(1)} %dynamic-slice_bitcast_fusion), channel_id=1, source_target_pairs={{0,2},{2,0},{1,3},{3,1},{4,6},{6,4},{5,7},{7,5},{8,10},{10,8},{9,1... | collective-permute-start | bytes 307208 | tf_op jit(solution)/shard_map/ppermute | solution.py:25
  15.5 1.1 %fusion.1 = bf16[4,8,3360]{2,1,0:T(8,128)(2,1)S(1)} fusion(bf16[2,8,8,3360]{3,2,0,1:T(8,128)(2,1)} %bitcast.36, bf16[2,8,8,3360]{3,2,0,1:T(8,128)(2,1)} %bitcast.37, pred[]{:T(512)S(6)} %eq.12), kind=kLoop, calls=%fused_computation.8 | loop fusion | flops 322560 | bytes 1935361 | tf_op jit(solution)/shard_map/jit(_where)/select_n | solution.py:32
  16.6 0.2 collective-permute-start.4
  16.7 2.0 %collective-permute-done = f32[40,640]{1,0:T(8,128)S(1)} collective-permute-done((f32[40,640]{1,0:T(8,128)S(1)}, f32[40,640]{1,0:T(8,128)S(1)}, u32[]{:S(2)}, u32[]{:S(2)}) %collective-permute-start) | collective-permute-done | bytes 102432 | tf_op jit(solution)/shard_map/ppermute | solution.py:25
  18.8 3.0 %collective-permute-start.1 = (bf16[40,640]{1,0:T(8,128)(2,1)S(1)}, bf16[40,640]{1,0:T(8,128)(2,1)S(1)}, u32[]{:S(2)}, u32[]{:S(2)}) collective-permute-start(bf16[40,640]{1,0:T(8,128)(2,1)S(1)} %get-tuple-element.8), channel_id=1, source_target_pairs={{0,4},{4,8},{8,12},{1,5},{5,9},{9,13},{2,6},{6,10},{10,14},{3,7},{... | collective-permute-start | bytes 153608 | tf_op jit(solution)/shard_map/ppermute | solution.py:20
  21.8 1.4 %copy_bitcast_fusion = (bf16[2,8,8,3360]{3,2,1,0:T(8,128)(2,1)S(1)}, bf16[2,8,8,3360]{3,2,1,0:T(8,128)(2,1)S(1)}) fusion(bf16[1,8,8,2,3360]{4,3,2,1,0:T(2,128)(2,1)} %copy-done.5, bf16[1,8,8,2,3360]{4,3,2,1,0:T(2,128)(2,1)S(1)} %get-tuple-element.10), kind=kLoop, calls=%fused_computation.1 | loop fusion | bytes 3440640 | tf_op jit(solution)/shard_map/transpose | solution.py:302
  23.2 9.2 %collective-permute-done.1 = bf16[40,640]{1,0:T(8,128)(2,1)S(1)} collective-permute-done((bf16[40,640]{1,0:T(8,128)(2,1)S(1)}, bf16[40,640]{1,0:T(8,128)(2,1)S(1)}, u32[]{:S(2)}, u32[]{:S(2)}) %collective-permute-start.1) | collective-permute-done | bytes 51232 | tf_op jit(solution)/shard_map/ppermute | solution.py:20
  32.4 5.6 %collective-permute-start.2 = (bf16[40,640]{1,0:T(8,128)(2,1)S(1)}, bf16[40,640]{1,0:T(8,128)(2,1)S(1)}, u32[]{:S(2)}, u32[]{:S(2)}) collective-permute-start(bf16[40,640]{1,0:T(8,128)(2,1)S(1)} %fusion.4), channel_id=1, source_target_pairs={{0,8},{4,12},{1,9},{5,13},{2,10},{6,14},{3,11},{7,15},{16,24},{20,... | collective-permute-start | bytes 153608 | tf_op jit(solution)/shard_map/ppermute | solution.py:20
  38.0 0.1 add_convert_fusion.flags
  38.1 1.7 %collective-permute-done.2 = bf16[40,640]{1,0:T(8,128)(2,1)S(1)} collective-permute-done((bf16[40,640]{1,0:T(8,128)(2,1)S(1)}, bf16[40,640]{1,0:T(8,128)(2,1)S(1)}, u32[]{:S(2)}, u32[]{:S(2)}) %collective-permute-start.2) | collective-permute-done | bytes 51232 | tf_op jit(solution)/shard_map/ppermute | solution.py:20
  39.8 1.6 %collective-permute-start.3 = (f32[40,640]{1,0:T(8,128)S(1)}, f32[40,640]{1,0:T(8,128)S(1)}, u32[]{:S(2)}, u32[]{:S(2)}) collective-permute-start(f32[40,640]{1,0:T(8,128)S(1)} %get-tuple-element.7), channel_id=1, source_target_pairs={{0,2},{2,0},{1,3},{3,1},{4,6},{6,4},{5,7},{7,5},{8,10},{10,8},{9,1... | collective-permute-start | bytes 307208 | tf_op jit(solution)/shard_map/ppermute | solution.py:25
  41.4 1.0 %fusion.3 = bf16[2,8,3360]{2,1,0:T(8,128)(2,1)S(1)} fusion(bf16[2,8,8,3360]{3,2,0,1:T(8,128)(2,1)} %collective-permute-done.5, pred[]{:T(512)S(6)} %eq.12), kind=kLoop, calls=%fused_computation.12 | loop fusion | flops 53760 | bytes 322561 | tf_op jit(solution)/shard_map/jit(_where)/select_n | solution.py:32
  42.3 0.6 collective-permute-start.6
  42.9 1.0 %fusion.7 = (bf16[2,8,3360]{2,1,0:T(8,128)(2,1)S(1)}, bf16[2,8,3360]{2,1,0:T(8,128)(2,1)S(1)}) fusion(bf16[4,8,3360]{2,1,0:T(8,128)(2,1)} %collective-permute-done.4), kind=kLoop, calls=%fused_computation.23 | loop fusion | bytes 430080 | tf_op jit(solution)/shard_map/slice | solution.py:306
  43.9 3.3 %own_conv.1 = (bf16[2,8,8,3360]{3,2,1,0:T(8,128)(2,1)S(1)}, bf16[2,8,8,3360]{3,2,1,0:T(8,128)(2,1)S(1)}) custom-call(s32[2]{0:T(128)S(1)} %add_convert_fusion.flags, bf16[2,8,8,3360]{3,2,1,0:T(8,128)(2,1)S(1)} %get-tuple-element.15.f0, bf16[2,8,8,3360]{3,2,1,0:T(8,128)(2,1)S(1)} %get-tuple-element.14.f1, ...), custom_call_target="tpu_custom_call" | custom-call | tf_op jit(solution)/shard_map/own_conv/pallas_call | solution.py:170
  47.2 0.7 %first_frame.1 = bf16[8,8,3360]{2,1,0:T(8,128)(2,1)S(1)} custom-call(bf16[2,8,8,3360]{3,2,1,0:T(8,128)(2,1)S(1)} %get-tuple-element.4.s0.near0, f32[3,2,3360]{2,1,0:T(2,128)S(1)} %copy-done.1), custom_call_target="tpu_custom_call" | custom-call | tf_op jit(solution)/shard_map/first_frame/pallas_call | solution.py:192
  47.9 1.2 %copy.12.raw = bf16[2,8,8,3360]{3,2,1,0:T(8,128)(2,1)S(1)} copy(bf16[2,8,8,3360]{3,2,0,1:T(8,128)(2,1)} %collective-permute-done.5) | data formatting | bytes 1720320 | tf_op jit(solution)/shard_map/ppermute | solution.py:20
  49.2 3.2 %mix_after.1 = bf16[8,8,3360]{2,1,0:T(8,128)(2,1)S(1)} custom-call(s32[2]{0:T(128)S(1)} %add_convert_fusion.flags, bf16[2,8,8,3360]{3,2,1,0:T(8,128)(2,1)S(1)} %copy.12.raw, bf16[2,8,3360]{2,1,0:T(8,128)(2,1)S(1)} %collective-permute-done.6.top.bottom, bf16[2,8,3360]{2,1,0:T(8,128)(2,1)S(1)} %collective-permute-done.6.top.bottom, ...), custom_call_target="tpu_custom_call" | custom-call | tf_op jit(solution)/shard_map/mix_after/pallas_call | solution.py:181
  52.4 4.4 %collective-permute-start.7 = (bf16[8,8,3360]{2,1,0:T(8,128)(2,1)S(1)}, bf16[8,8,3360]{2,1,0:T(8,128)(2,1)S(1)}, u32[]{:S(2)}, u32[]{:S(2)}) collective-permute-start(bf16[8,8,3360]{2,1,0:T(8,128)(2,1)S(1)} %mix_after.1), channel_id=1, source_target_pairs={{0,4},{4,8},{8,12},{1,5},{5,9},{9,13},{2,6},{6,10},{10,14},{3,7},{... | collective-permute-start | bytes 1290248 | tf_op jit(solution)/shard_map/ppermute | solution.py:20
  56.8 1.0 %fusion.2 = bf16[2,8,3360]{2,1,0:T(8,128)(2,1)S(1)} fusion(bf16[2,8,8,3360]{3,2,0,1:T(8,128)(2,1)} %collective-permute-done.8, pred[]{:T(512)S(6)} %eq.12), kind=kLoop, calls=%fused_computation.10 | loop fusion | flops 53760 | bytes 322561 | tf_op jit(solution)/shard_map/jit(_where)/select_n | solution.py:32
  57.8 1.6 %collective-permute-start.9 = (bf16[2,8,3360]{2,1,0:T(8,128)(2,1)S(1)}, bf16[2,8,3360]{2,1,0:T(8,128)(2,1)S(1)}, u32[]{:S(2)}, u32[]{:S(2)}) collective-permute-start(bf16[2,8,3360]{2,1,0:T(8,128)(2,1)S(1)} %fusion.2), channel_id=1, source_target_pairs={{0,2},{2,0},{1,3},{3,1},{4,6},{6,4},{5,7},{7,5},{8,10},{10,8},{9,1... | collective-permute-start | bytes 322568 | tf_op jit(solution)/shard_map/ppermute | solution.py:32
  59.4 1.4 %attend.1 = bf16[128,1120]{1,0:T(8,128)(2,1)} custom-call(bf16[128,1120]{1,0:T(8,128)(2,1)S(1)} %bitcast.41, f32[2,40,640]{2,1,0:T(8,128)S(1)} %bitcast_dynamic-update-slice_fusion.state), custom_call_target="tpu_custom_call" | custom-call | tf_op jit(solution)/shard_map/attend/pallas_call | solution.py:268
  60.8 1.2 %copy.13.raw = bf16[2,8,8,3360]{3,2,1,0:T(8,128)(2,1)S(1)} copy(bf16[2,8,8,3360]{3,2,0,1:T(8,128)(2,1)} %collective-permute-done.8) | data formatting | bytes 1720320 | tf_op jit(solution)/shard_map/ppermute | solution.py:20
  62.0 0.6 collective-permute-done.9.top.bottom
  62.6 3.2 %mix_before.1 = bf16[8,8,3360]{2,1,0:T(8,128)(2,1)S(1)} custom-call(s32[2]{0:T(128)S(1)} %add_convert_fusion.flags, bf16[2,8,8,3360]{3,2,1,0:T(8,128)(2,1)S(1)} %copy.13.raw, bf16[2,8,3360]{2,1,0:T(8,128)(2,1)S(1)} %collective-permute-done.9.top.bottom, bf16[2,8,3360]{2,1,0:T(8,128)(2,1)S(1)} %collective-permute-done.9.top.bottom, ...), custom_call_target="tpu_custom_call" | custom-call | tf_op jit(solution)/shard_map/mix_before/pallas_call | solution.py:181
  65.9 1.0 %pad_maximum_fusion = bf16[2,8,8,3360]{3,2,1,0:T(8,128)(2,1)} fusion(bf16[1,8,8,3360]{3,2,1,0:T(8,128)(2,1)S(1)} %bitcast.38, bf16[1,8,8,3360]{3,2,1,0:T(8,128)(2,1)S(1)} %select_bitcast_fusion), kind=kLoop, calls=%fused_computation | loop fusion | flops 430080 | bytes 1720320 | tf_op jit(solution)/shard_map/stack | solution.py:324
  (24 shorter events, 0.2 us)
Async XLA Ops:
  3.3 3.3 %copy-start.5 = (bf16[1,8,8,2,3360]{4,3,2,1,0:T(2,128)(2,1)}, bf16[1,8,8,2,3360]{4,3,2,1,0:T(2,128)(2,1)S(1)}, u32[]{:S(2)}) copy-start(bf16[1,8,8,2,3360]{4,3,2,1,0:T(2,128)(2,1)S(1)} %get-tuple-element.11) | copy-start | bytes 2580484
  3.3 9.8 %copy-start.2 = (bf16[2,8,8,1120]{3,2,1,0:T(8,128)(2,1)S(1)}, bf16[2,8,8,1120]{3,2,1,0:T(8,128)(2,1)}, u32[]{:S(2)}) copy-start(bf16[2,8,8,1120]{3,2,1,0:T(8,128)(2,1)} %param.7) | copy-start | bytes 860164
  3.3 9.8 %copy-start.3 = (bf16[2,8,8,1120]{3,2,1,0:T(8,128)(2,1)S(1)}, bf16[2,8,8,1120]{3,2,1,0:T(8,128)(2,1)}, u32[]{:S(2)}) copy-start(bf16[2,8,8,1120]{3,2,1,0:T(8,128)(2,1)} %param.8) | copy-start | bytes 860164
  4.3 37.0 %collective-permute-start.5 = (bf16[2,8,8,3360]{3,2,0,1:T(8,128)(2,1)}, bf16[2,8,8,3360]{3,2,0,1:T(8,128)(2,1)}, u32[]{:S(2)}, u32[]{:S(2)}) collective-permute-start(bf16[2,8,8,3360]{3,2,0,1:T(8,128)(2,1)} %bitcast.37), channel_id=1, source_target_pairs={{4,0},{8,4},{12,8},{5,1},{9,5},{13,9},{6,2},{10,6},{14,10},{7,3},{... | collective-permute-start | bytes 2580488 | tf_op jit(solution)/shard_map/ppermute | solution.py:20
  6.6 50.2 %collective-permute-start.8 = (bf16[2,8,8,3360]{3,2,0,1:T(8,128)(2,1)}, bf16[2,8,8,3360]{3,2,0,1:T(8,128)(2,1)}, u32[]{:S(2)}, u32[]{:S(2)}) collective-permute-start(bf16[2,8,8,3360]{3,2,0,1:T(8,128)(2,1)} %bitcast.36), channel_id=1, source_target_pairs={{0,4},{4,8},{8,12},{1,5},{5,9},{9,13},{2,6},{6,10},{10,14},{3,7},{... | collective-permute-start | bytes 2580488 | tf_op jit(solution)/shard_map/ppermute | solution.py:20
  13.5 5.3 %collective-permute-start = (f32[40,640]{1,0:T(8,128)S(1)}, f32[40,640]{1,0:T(8,128)S(1)}, u32[]{:S(2)}, u32[]{:S(2)}) collective-permute-start(f32[40,640]{1,0:T(8,128)S(1)} %dynamic-slice_bitcast_fusion), channel_id=1, source_target_pairs={{0,2},{2,0},{1,3},{3,1},{4,6},{6,4},{5,7},{7,5},{8,10},{10,8},{9,1... | collective-permute-start | bytes 307208 | tf_op jit(solution)/shard_map/ppermute | solution.py:25
  16.6 26.4 %collective-permute-start.4 = (bf16[4,8,3360]{2,1,0:T(8,128)(2,1)S(1)}, bf16[4,8,3360]{2,1,0:T(8,128)(2,1)}, u32[]{:S(2)}, u32[]{:S(2)}) collective-permute-start(bf16[4,8,3360]{2,1,0:T(8,128)(2,1)S(1)} %fusion.1), channel_id=1, source_target_pairs={{0,2},{2,0},{1,3},{3,1},{4,6},{6,4},{5,7},{7,5},{8,10},{10,8},{9,1... | collective-permute-start | bytes 645128 | tf_op jit(solution)/shard_map/ppermute | solution.py:32
  18.7 25.2 %copy-start = (f32[3,3,2,3360]{3,2,1,0:T(2,128)S(1)}, f32[3,3,2,3360]{3,2,1,0:T(2,128)}, u32[]{:S(2)}) copy-start(f32[3,3,2,3360]{3,2,1,0:T(2,128)} %weight.5) | copy-start | bytes 725764
  18.8 13.6 %collective-permute-start.1 = (bf16[40,640]{1,0:T(8,128)(2,1)S(1)}, bf16[40,640]{1,0:T(8,128)(2,1)S(1)}, u32[]{:S(2)}, u32[]{:S(2)}) collective-permute-start(bf16[40,640]{1,0:T(8,128)(2,1)S(1)} %get-tuple-element.8), channel_id=1, source_target_pairs={{0,4},{4,8},{8,12},{1,5},{5,9},{9,13},{2,6},{6,10},{10,14},{3,7},{... | collective-permute-start | bytes 153608 | tf_op jit(solution)/shard_map/ppermute | solution.py:20
  32.4 7.4 %collective-permute-start.2 = (bf16[40,640]{1,0:T(8,128)(2,1)S(1)}, bf16[40,640]{1,0:T(8,128)(2,1)S(1)}, u32[]{:S(2)}, u32[]{:S(2)}) collective-permute-start(bf16[40,640]{1,0:T(8,128)(2,1)S(1)} %fusion.4), channel_id=1, source_target_pairs={{0,8},{4,12},{1,9},{5,13},{2,10},{6,14},{3,11},{7,15},{16,24},{20,... | collective-permute-start | bytes 153608 | tf_op jit(solution)/shard_map/ppermute | solution.py:20
  38.1 9.1 %copy-start.1 = (f32[3,2,3360]{2,1,0:T(2,128)S(1)}, f32[3,2,3360]{2,1,0:T(2,128)}, u32[]{:S(2)}) copy-start(f32[3,2,3360]{2,1,0:T(2,128)} %temporal.5) | copy-start | bytes 241924
  39.8 19.5 %collective-permute-start.3 = (f32[40,640]{1,0:T(8,128)S(1)}, f32[40,640]{1,0:T(8,128)S(1)}, u32[]{:S(2)}, u32[]{:S(2)}) collective-permute-start(f32[40,640]{1,0:T(8,128)S(1)} %get-tuple-element.7), channel_id=1, source_target_pairs={{0,2},{2,0},{1,3},{3,1},{4,6},{6,4},{5,7},{7,5},{8,10},{10,8},{9,1... | collective-permute-start | bytes 307208 | tf_op jit(solution)/shard_map/ppermute | solution.py:25
  42.3 6.8 %collective-permute-start.6 = (bf16[2,8,3360]{2,1,0:T(8,128)(2,1)S(1)}, bf16[2,8,3360]{2,1,0:T(8,128)(2,1)S(1)}, u32[]{:S(2)}, u32[]{:S(2)}) collective-permute-start(bf16[2,8,3360]{2,1,0:T(8,128)(2,1)S(1)} %fusion.3), channel_id=1, source_target_pairs={{0,2},{2,0},{1,3},{3,1},{4,6},{6,4},{5,7},{7,5},{8,10},{10,8},{9,1... | collective-permute-start | bytes 322568 | tf_op jit(solution)/shard_map/ppermute | solution.py:32
  49.1 10.2 %copy-start.4 = (bf16[2,8,8,1120]{3,2,1,0:T(8,128)(2,1)S(1)}, bf16[2,8,8,1120]{3,2,1,0:T(8,128)(2,1)}, u32[]{:S(2)}) copy-start(bf16[2,8,8,1120]{3,2,1,0:T(8,128)(2,1)} %param.6) | copy-start | bytes 860164
  52.4 13.4 %collective-permute-start.7 = (bf16[8,8,3360]{2,1,0:T(8,128)(2,1)S(1)}, bf16[8,8,3360]{2,1,0:T(8,128)(2,1)S(1)}, u32[]{:S(2)}, u32[]{:S(2)}) collective-permute-start(bf16[8,8,3360]{2,1,0:T(8,128)(2,1)S(1)} %mix_after.1), channel_id=1, source_target_pairs={{0,4},{4,8},{8,12},{1,5},{5,9},{9,13},{2,6},{6,10},{10,14},{3,7},{... | collective-permute-start | bytes 1290248 | tf_op jit(solution)/shard_map/ppermute | solution.py:20
  57.8 4.8 %collective-permute-start.9 = (bf16[2,8,3360]{2,1,0:T(8,128)(2,1)S(1)}, bf16[2,8,3360]{2,1,0:T(8,128)(2,1)S(1)}, u32[]{:S(2)}, u32[]{:S(2)}) collective-permute-start(bf16[2,8,3360]{2,1,0:T(8,128)(2,1)S(1)} %fusion.2), channel_id=1, source_target_pairs={{0,2},{2,0},{1,3},{3,1},{4,6},{6,4},{5,7},{7,5},{8,10},{10,8},{9,1... | collective-permute-start | bytes 322568 | tf_op jit(solution)/shard_map/ppermute | solution.py:32

commit v2 on v1

v2 whole, which is shorter than its diff:
```python
import functools

import jax
import jax.numpy as jnp
from jax import lax
from jax.experimental import pallas as pl
from jax.experimental.pallas import tpu as pltpu
from jax.sharding import PartitionSpec as P

HEAD_DIM = 32
LANES = 128
STATE_ROWS = HEAD_DIM + 8
BLOCK = 8
SENT_ROWS = 5
F32 = jnp.float32
BF16 = jnp.bfloat16


def permuted(value, axis, pairs):
    return lax.ppermute(value, axis, pairs)


def shifted(value, axis, steps):
    count = lax.axis_size(axis)
    first, last = (max(0, -steps), min(count, count - steps))
    return permuted(value, axis, [(source, source + steps) for source in range(first, last)])


def rotated(value, axis, steps):
    count = lax.axis_size(axis)
    return permuted(value, axis, [(source, (source + steps) % count) for source in range(count)])


VMEM = pl.BlockSpec(memory_space=pltpu.VMEM)
SMEM = pl.BlockSpec(memory_space=pltpu.SMEM)
ANY = pl.BlockSpec(memory_space=pl.ANY)


def kernel_call(kernel, out_shape, operands, specs=None, out_specs=None, scratch=(), aliases=None, vmem_mib=16):
    many = isinstance(out_shape, tuple)
    return pl.pallas_call(
        kernel,
        out_shape=out_shape,
        in_specs=[VMEM] * len(operands) if specs is None else specs,
        out_specs=out_specs if out_specs is not None else ((VMEM,) * len(out_shape) if many else VMEM),
        scratch_shapes=scratch,
        input_output_aliases=aliases or {},
        compiler_params=pltpu.CompilerParams(vmem_limit_bytes=vmem_mib << 20),
    )(*operands)


def lane_tiles(channels, body):
    full = channels // LANES

    @pl.loop(0, full)
    def _(tile):
        body(pl.ds(pl.multiple_of(tile * LANES, LANES), LANES), LANES)

    if channels % LANES:
        body(pl.ds(full * LANES, channels % LANES), channels % LANES)


def spread(row, columns, width):
    return jnp.broadcast_to(row, (columns, width))


def tap_weights(weight_ref, part, lanes, width, columns):
    column = lax.broadcasted_iota(jnp.int32, (columns, width), 0)
    taps = []
    for row_tap in range(3):
        row = []
        for col_tap in range(3):
            w = spread(weight_ref[row_tap, col_tap, part : part + 1, lanes], columns, width)
            if col_tap == 0:
                w = jnp.where(column == columns - 1, 0.0, w)
            if col_tap == 2:
                w = jnp.where(column == 0, 0.0, w)
            row.append(w)
        taps.append(row)
    return taps


def conv_row(above, here, below, taps, columns):
    sums = [taps[0][b] * above + taps[1][b] * here + taps[2][b] * below for b in range(3)]
    total = sums[1] + pltpu.roll(sums[0], 1, 0) + pltpu.roll(sums[2], columns - 1, 0)
    return total.astype(BF16)


def conv_interior(load, wanted, taps, columns):
    held = {}

    def row(r):
        if r not in held:
            held[r] = load(r)
        return held[r]

    return [conv_row(row(r - 1), row(r), row(r + 1), taps, columns) for r in wanted]


def interior_kernel(jobs, frames, weight, out):
    columns, channels = frames.shape[3:]

    def tile(lanes, width):
        for part in range(2):
            taps = tap_weights(weight, part, lanes, width, columns)
            at = 0
            for frame, wanted in jobs:

                def load(r, frame=frame, part=part):
                    return frames[frame, r, part, :, lanes].astype(F32)

                for value in conv_interior(load, wanted, taps, columns):
                    out[at, part, :, lanes] = value
                    at += 1

    lane_tiles(channels, tile)


def interior(frames, weight, jobs):
    rows = sum(len(wanted) for _, wanted in jobs)
    return kernel_call(
        functools.partial(interior_kernel, jobs),
        jax.ShapeDtypeStruct((rows,) + frames.shape[2:], BF16),
        (frames, weight),
    )


def slab_places(chunk, channels):
    per_slab = channels // chunk
    return [(block // per_slab, block % per_slab * chunk) for block in range(STATE_ROWS // BLOCK)]


def pack_kernel(edges, index, frames, state, out):
    row_count, _, columns, channels = frames.shape[1:]
    chunk = state.shape[2]
    at = 0
    if edges is not None:
        for frame in range(2):
            for part in range(2):
                if edges == "either":
                    first = index[1] == 0

                    @pl.when(first)
                    def _(frame=frame, part=part, at=at):
                        out[at] = frames[frame, row_count - 1, part]

                    @pl.when(jnp.logical_not(first))
                    def _(frame=frame, part=part, at=at):
                        out[at] = frames[frame, 0, part]

                else:
                    out[at] = frames[frame, 0 if edges == "head" else row_count - 1, part]
                at += 1
    places = slab_places(chunk, channels)
    for slab in range(places[-1][0] + 1):
        out[at + slab] = jnp.zeros((columns, channels), BF16)
    for block, (slab, lane) in enumerate(places):
        out[at + slab, :, lane : lane + chunk] = state[
            index[0], block * BLOCK : (block + 1) * BLOCK, :
        ].astype(BF16)


def boundary_kernel(n_packs, first_of, top_at, bottom_at, info, frames, weight, state, *refs):
    packs, (out, total) = (refs[:n_packs], refs[n_packs:])
    row_count, _, columns, channels = frames.shape[1:]
    has_top, has_bottom = (info[0].astype(F32), info[1].astype(F32))
    chunk = state.shape[2]

    def tile(lanes, width):
        for part in range(2):
            taps = tap_weights(weight, part, lanes, width, columns)
            for frame in range(2):

                def load(r, frame=frame, part=part):
                    if r < 0:
                        return packs[top_at][2 * frame + part, :, lanes].astype(F32) * has_top
                    if r == row_count:
                        return packs[bottom_at][2 * frame + part, :, lanes].astype(F32) * has_bottom
                    return frames[frame, r, part, :, lanes].astype(F32)

                for i, value in enumerate(conv_interior(load, (0, row_count - 1), taps, columns)):
                    out[2 * frame + i, part, :, lanes] = value

    lane_tiles(channels, tile)
    for block, (slab, lane) in enumerate(slab_places(chunk, channels)):
        rows = slice(block * BLOCK, (block + 1) * BLOCK)
        value = state[info[2], rows, :]
        for pack, first in zip(packs, first_of):
            value = value + pack[first + slab, :, lane : lane + chunk].astype(F32)
        total[rows, :] = value


def gate(value, key):
    return value * (key / (1.0 + jnp.exp(-key)))


def theirs_kernel(raw, s0, s1, weight, temporal, out):
    columns, channels = raw.shape[2:]
    count = out.shape[0]

    def tile(lanes, width):
        mixed = []
        for part in range(2):
            taps = tap_weights(weight, part, lanes, width, columns)
            w = [spread(temporal[tap, part : part + 1, lanes], columns, width) for tap in range(3)]

            def load(r, part=part):
                return raw[r, part, :, lanes].astype(F32)

            mixed.append(
                [
                    w[0] * s0[r, part, :, lanes].astype(F32)
                    + w[1] * s1[r, part, :, lanes].astype(F32)
                    + w[2] * value.astype(F32)
                    for r, value in enumerate(conv_interior(load, range(1, count + 1), taps, columns))
                ]
            )
        for r in range(count):
            out[r, :, lanes] = gate(mixed[0][r], mixed[1][r]).astype(BF16)

    lane_tiles(channels, tile)


def ours_kernel(sent, info, mine_a, mine_b, mine_s0, before_a, before_b, temporal, out, frame0, frame1, sems):
    row_count, columns, channels = frame1.shape
    inner = row_count - 2

    def spatial(a, b, frame, r, part, lanes):
        if r in (0, row_count - 1):
            ref, at = (b, 2 * frame + (r > 0))
        elif frame == 1:
            ref, at = (a, r - 1)
        elif r > sent:
            ref, at = (a, inner + r - sent - 1)
        else:
            ref, at = (mine_s0, r - 1)
        return ref[at, part, :, lanes].astype(F32)

    def weights(lanes, width):
        return [
            [spread(temporal[tap, part : part + 1, lanes], columns, width) for tap in range(3)]
            for part in range(2)
        ]

    def tile(lanes, width):
        w = weights(lanes, width)
        for r in range(row_count):
            late = [
                [
                    spatial(before_a, before_b, 1, r, part, lanes),
                    spatial(mine_a, mine_b, 0, r, part, lanes),
                    spatial(mine_a, mine_b, 1, r, part, lanes),
                ]
                for part in range(2)
            ]
            mixed = [w[p][0] * late[p][0] + w[p][1] * late[p][1] + w[p][2] * late[p][2] for p in range(2)]
            frame1[r, :, lanes] = gate(*mixed).astype(BF16)
            if not 1 <= r <= sent:
                mixed = [
                    w[p][0] * spatial(before_a, before_b, 0, r, p, lanes)
                    + w[p][1] * late[p][0]
                    + w[p][2] * late[p][1]
                    for p in range(2)
                ]
                frame0[r, :, lanes] = gate(*mixed).astype(BF16)

    lane_tiles(channels, tile)

    @pl.when(info[3] == 1)
    def _():
        def first_tile(lanes, width):
            w = weights(lanes, width)
            for r in range(1, sent + 1):
                mixed = [w[p][2] * mine_s0[r - 1, p, :, lanes].astype(F32) for p in range(2)]
                frame0[r, :, lanes] = gate(*mixed).astype(BF16)

        lane_tiles(channels, first_tile)

    copies = [
        pltpu.make_async_copy(frame0, out.at[0], sems.at[0]),
        pltpu.make_async_copy(frame1, out.at[1], sems.at[1]),
    ]
    for copy in copies:
        copy.start()
    for copy in copies:
        copy.wait()


def place_kernel(info, rows, gated, out, sem):
    @pl.when(info[3] == 0)
    def _():
        copy = pltpu.make_async_copy(rows, out.at[0, pl.ds(1, rows.shape[0])], sem)
        copy.start()
        copy.wait()


def head_mask(width):
    row = lax.broadcasted_iota(jnp.int32, (width, width), 0) // HEAD_DIM
    column = lax.broadcasted_iota(jnp.int32, (width, width), 1) // HEAD_DIM
    return row == column


def lane_groups(channels):
    return [(at, min(LANES, channels - at)) for at in range(0, channels, LANES)]


def state_kernel(key, value, state):
    tokens, channels = key.shape
    chunk = state.shape[2]
    ones = jnp.ones((8, tokens), BF16)
    state[...] = jnp.zeros_like(state)
    for at, width in lane_groups(channels):
        keys = jnp.maximum(key[:, at : at + width], 0)
        product = lax.dot_general(
            keys, value[:, at : at + width], (((0,), (0,)), ((), ())), preferred_element_type=F32
        )
        product = jnp.where(head_mask(width), product, 0.0)
        folded = sum(product[d : d + HEAD_DIM] for d in range(0, width, HEAD_DIM))
        lanes = slice(at % chunk, at % chunk + width)
        state[at // chunk, :HEAD_DIM, lanes] = folded
        state[at // chunk, HEAD_DIM:, lanes] = jnp.dot(ones, keys, preferred_element_type=F32)


def split(value):
    high = value.astype(BF16)
    return (high, (value - high.astype(F32)).astype(BF16))


def attend_kernel(query, state, out):
    channels = query.shape[1]
    chunk = state.shape[2]
    for at, width in lane_groups(channels):
        rows = jnp.maximum(query[:, at : at + width], 0)
        lanes = slice(at % chunk, at % chunk + width)
        mask = head_mask(width)
        folded = state[at // chunk, :HEAD_DIM, lanes]
        kv = jnp.where(mask, jnp.concatenate([folded] * (width // HEAD_DIM), axis=0), 0.0)
        sums = jnp.where(
            mask, jnp.broadcast_to(state[at // chunk, HEAD_DIM : HEAD_DIM + 1, lanes], (width, width)), 0.0
        )
        numerator = sum(jnp.dot(rows, part, preferred_element_type=F32) for part in split(kv))
        denominator = sum(
            lax.dot_general(rows, part, (((1,), (1,)), ((), ())), preferred_element_type=F32)
            for part in split(sums)
        )
        out[:, at : at + width] = (numerator / (denominator + 1.0)).astype(BF16)


def local_state(key, value, chunks):
    channels = key.shape[1]
    groups = pl.cdiv(pl.cdiv(channels, LANES), chunks)
    return kernel_call(state_kernel, jax.ShapeDtypeStruct((chunks, STATE_ROWS, groups * LANES), F32), (key, value))


def attend(query, state):
    return kernel_call(attend_kernel, jax.ShapeDtypeStruct(query.shape, BF16), (query, state))


def layer(query_proj, key_proj, value_proj, expanded, spatial_weight, temporal_weight):
    frames, row_count, col_count, channels = query_proj.shape
    hidden = expanded.shape[4]
    assert frames == 2 and row_count >= 4
    sent = SENT_ROWS if row_count == 8 else row_count - 2
    space, spaces = (lax.axis_index("space"), lax.axis_size("space"))
    info = jnp.stack(
        [space > 0, space < spaces - 1, space, lax.axis_index("tm") == 0]
    ).astype(jnp.int32)

    def tokens(array):
        return array.reshape(-1, channels)

    held = lax.optimization_barrier(jnp.transpose(expanded, (0, 1, 3, 2, 4)))
    after = shifted(held[0, : sent + 2], "tm", -1)

    mine_a = interior(
        held, spatial_weight, ((1, tuple(range(1, row_count - 1))), (0, tuple(range(sent + 1, row_count - 1))))
    )
    before_a = shifted(mine_a, "tm", 1)

    state = local_state(tokens(key_proj), tokens(value_proj), spaces)
    chunk = state.shape[2]
    slabs = slab_places(chunk, hidden)[-1][0] + 1
    packs, first_of, top_at, bottom_at = ([], [], None, None)
    for step in range(1, spaces):
        edges = "either" if spaces == 2 else {1: "tail", spaces - 1: "head"}.get(step)
        edge_rows = 4 if edges else 0
        if edges in ("tail", "either"):
            top_at = step - 1
        if edges in ("head", "either"):
            bottom_at = step - 1
        packed = kernel_call(
            functools.partial(pack_kernel, edges),
            jax.ShapeDtypeStruct((edge_rows + slabs, col_count, hidden), BF16),
            (jnp.stack([(space + step) % spaces, space]).astype(jnp.int32), held, state),
            [SMEM, VMEM, VMEM],
        )
        packs.append(rotated(packed, "space", step))
        first_of.append(edge_rows)

    mine_s0 = interior(held, spatial_weight, ((0, tuple(range(1, sent + 1))),))
    mine_b, own = kernel_call(
        functools.partial(boundary_kernel, len(packs), tuple(first_of), top_at, bottom_at),
        (
            jax.ShapeDtypeStruct((4, 2, col_count, hidden), BF16),
            jax.ShapeDtypeStruct((STATE_ROWS, chunk), F32),
        ),
        (info, held, spatial_weight, state, *packs),
        [SMEM] + [VMEM] * (3 + len(packs)),
    )
    step = 1
    while step < lax.axis_size("tm"):
        own = own + shifted(own.astype(BF16), "tm", step).astype(F32)
        step *= 2
    before_b = shifted(mine_b, "tm", 1)

    theirs = kernel_call(
        theirs_kernel,
        jax.ShapeDtypeStruct((sent, col_count, hidden), BF16),
        (after, mine_s0, mine_a, spatial_weight, temporal_weight),
    )
    returned = shifted(theirs, "tm", 1)

    whole = lax.dynamic_update_index_in_dim(state, own, space, 0)
    for step in range(1, spaces):
        whole = lax.dynamic_update_index_in_dim(whole, rotated(own, "space", step), (space - step) % spaces, 0)
    attended = attend(tokens(query_proj), whole).reshape(query_proj.shape)

    gated_shape = jax.ShapeDtypeStruct((2, row_count, col_count, hidden), BF16)
    gated = kernel_call(
        functools.partial(ours_kernel, sent),
        gated_shape,
        (info, mine_a, mine_b, mine_s0, before_a, before_b, temporal_weight),
        [SMEM] + [VMEM] * 6,
        ANY,
        [pltpu.VMEM(gated_shape.shape[1:], BF16)] * 2 + [pltpu.SemaphoreType.DMA((2,))],
    )
    gated = kernel_call(
        place_kernel, gated_shape, (info, returned, gated), [SMEM, VMEM, ANY], ANY, [pltpu.SemaphoreType.DMA], {2: 0}
    )
    return (attended, gated)


def solution(mesh):
    return jax.shard_map(
        layer,
        mesh=mesh,
        in_specs=(
            P(("groups", "tm"), "space", None, "mp"),
            P(("groups", "tm"), "space", None, "mp"),
            P(("groups", "tm"), "space", None, "mp"),
            P(("groups", "tm"), "space", None, None, "mp"),
            P(None, None, None, "mp"),
            P(None, None, "mp"),
        ),
        out_specs=(
            P(("groups", "tm"), "space", None, "mp"),
            P(("groups", "tm"), "space", None, "mp"),
        ),
        check_vma=False,
    )
```

time: 67.4 us -> 62 us (0.920)
  local copies, waits for them, and re-layouts: 9.55 us -> 4.45 us
  other arithmetic: 4.24 us -> 0.84 us
  waiting for transfers between devices: 13.4 us -> 16.6 us
  Pallas kernels: 12.1 us -> 14.8 us
  starting transfers between devices: 26.7 us -> 24 us
    slice x2 -> x0, local copies, waits for them, and re-layouts: 3.62 us -> none  [the longest x1 2.65 us: on_device(): f0, f1 = (jnp.transpose(expanded[t], (2, 0, 1, 3)) for t in range(2))]
    ppermute x10 -> x8, waiting for transfers between devices: 13.4 us -> 16.6 us  [permuted(): return lax.ppermute(value, axis, pairs)]
    select_n x3 -> x0, other arithmetic: 3.04 us -> none  [edge_rows(): jnp.where(mine == 0, tail, head)]
    ppermute x10 -> x8, starting transfers between devices: 26.7 us -> 24 us  [permuted(): return lax.ppermute(value, axis, pairs)]
    pallas_call x6 -> x9, Pallas kernels: 12.1 us -> 14.8 us  [kernel_call(): pl.pallas_call(kernel, out_shape=out_shape, in_specs=[VMEM] * len(operand...]
    ppermute x2 -> x0, local copies, waits for them, and re-layouts: 2.46 us -> none  [shifted(): lax.ppermute(value, axis, [(source, source + steps) for source in range(f...]
    transpose x1 -> x0, local copies, waits for them, and re-layouts: 1.41 us -> none  [on_device(): f0, f1 = (jnp.transpose(expanded[t], (2, 0, 1, 3)) for t in range(2))]
    squeeze x1, local copies, waits for them, and re-layouts: 0.02 us -> 0.93 us  [layer(): after = shifted(held[0, :sent + 2], 'tm', -1)]
  transfers between devices with their start and end apart: 10 -> 8, of which waited for: 4 -> 2; matrix products, arithmetic and copies ran while one was open for 14% -> 4% of each run, Pallas kernels for 18% -> 22%
where the time goes in v2:
time: 62 us; the launch traced here: 61.6 us
  starting transfers between devices  24 us (39%)
  waiting for transfers between devices  16.6 us (27%)
  Pallas kernels  14.8 us (24%)
  local copies, waits for them, and re-layouts  4.45 us (7%)
  other arithmetic  0.84 us (1%)
  between operations  0.83 us (1%)
    ppermute x8, starting transfers between devices, permuted(): return lax.ppermute(value, axis, pairs)  24 us
    ppermute x8, waiting for transfers between devices, permuted(): return lax.ppermute(value, axis, pairs)  16.6 us
    pallas_call x9, Pallas kernels, kernel_call(): pl.pallas_call(kernel, out_shape=out_shape, in_specs=[VMEM] * len(operand...  14.8 us
    unnamed x13, local copies, waits for them, and re-layouts  2.61 us
  transfers between devices with their start and end apart: 8, of which 2 were waited for; matrix products, arithmetic and copies ran while one was open for 4% of the time, Pallas kernels for 22%

profile of v2, /device:TPU:0, one launch (start us, length us, event | category | flops | bytes accessed | tf_op | source)
XLA Modules:
  0.0 61.6 jit_solution(1131336144958933667)
XLA Ops:
  0.7 1.7 %copy.11 = bf16[2,8,8,2,3360]{4,2,3,1,0:T(8,128)(2,1)S(1)} copy(bf16[2,8,8,2,3360]{4,3,2,1,0:T(2,128)(2,1)} %param.9) | data formatting | bytes 3440640 | tf_op args[3]
  2.4 0.3 shard_map.77.state
  2.7 0.1 pad_add_fusion.1.index
  2.8 0.6 shard_map.78
  3.4 3.0 %collective-permute-start = (bf16[5,8,3360]{2,1,0:T(8,128)(2,1)S(1)}, bf16[5,8,3360]{2,1,0:T(8,128)(2,1)S(1)}, u32[]{:S(2)}, u32[]{:S(2)}) collective-permute-start(bf16[5,8,3360]{2,1,0:T(8,128)(2,1)S(1)} %shard_map.78), channel_id=1, source_target_pairs={{0,2},{2,0},{1,3},{3,1},{4,6},{6,4},{5,7},{7,5},{8,10},{10,8},{9,1... | collective-permute-start | bytes 806408 | tf_op jit(solution)/shard_map/ppermute | solution.py:20
  6.5 0.9 %slice_bitcast_fusion = bf16[7,2,8,3360]{3,2,1,0:T(8,128)(2,1)} fusion(bf16[2,8,2,8,3360]{4,3,2,1,0:T(8,128)(2,1)S(1)} %bitcast.19), kind=kLoop, calls=%fused_computation.1 | loop fusion | bytes 1505280 | tf_op jit(solution)/shard_map/squeeze | solution.py:373
  7.4 1.3 %collective-permute-start.4 = (bf16[7,2,8,3360]{3,2,1,0:T(8,128)(2,1)}, bf16[7,2,8,3360]{3,2,1,0:T(8,128)(2,1)}, u32[]{:S(2)}, u32[]{:S(2)}) collective-permute-start(bf16[7,2,8,3360]{3,2,1,0:T(8,128)(2,1)} %slice_bitcast_fusion), channel_id=1, source_target_pairs={{4,0},{8,4},{12,8},{5,1},{9,5},{13,9},{6,2},{10,6},{14,10},{7,3},{... | collective-permute-start | bytes 2257928 | tf_op jit(solution)/shard_map/ppermute | solution.py:20
  8.7 0.1 pad_add_fusion.info
  8.8 4.3 %collective-permute-done.refs_0_ = bf16[5,8,3360]{2,1,0:T(8,128)(2,1)S(1)} collective-permute-done((bf16[5,8,3360]{2,1,0:T(8,128)(2,1)S(1)}, bf16[5,8,3360]{2,1,0:T(8,128)(2,1)S(1)}, u32[]{:S(2)}, u32[]{:S(2)}) %collective-permute-start) | collective-permute-done | bytes 268832 | tf_op jit(solution)/shard_map/ppermute | solution.py:20
  13.1 2.3 %shard_map.79 = (bf16[4,2,8,3360]{3,2,1,0:T(8,128)(2,1)}, f32[40,640]{1,0:T(8,128)S(1)}) custom-call(s32[4]{0:T(128)S(1)} %pad_add_fusion.info, bf16[2,8,2,8,3360]{4,3,2,1,0:T(8,128)(2,1)S(1)} %bitcast.20, f32[3,3,2,3360]{3,2,1,0:T(2,128)S(1)} %copy-done, f32[2,40,640]{2,1,0:T(8,128)S(1)} %shard_map.77.state, ...), custom_call_target="tpu_custom_call" | custom-call | tf_op jit(solution)/shard_map/pallas_call | solution.py:41
  15.4 3.7 %collective-permute-start.1 = (bf16[40,640]{1,0:T(8,128)(2,1)S(1)}, bf16[40,640]{1,0:T(8,128)(2,1)S(1)}, u32[]{:S(2)}, u32[]{:S(2)}) collective-permute-start(bf16[40,640]{1,0:T(8,128)(2,1)S(1)} %convert_element_type.15), channel_id=1, source_target_pairs={{0,4},{4,8},{8,12},{1,5},{5,9},{9,13},{2,6},{6,10},{10,14},{3,7},{... | collective-permute-start | bytes 153608 | tf_op jit(solution)/shard_map/ppermute | solution.py:20
  19.1 1.4 %shard_map.82.s1.mine_a = bf16[7,2,8,3360]{3,2,1,0:T(8,128)(2,1)S(1)} custom-call(bf16[2,8,2,8,3360]{4,3,2,1,0:T(8,128)(2,1)S(1)} %bitcast.21, f32[3,3,2,3360]{3,2,1,0:T(2,128)S(1)} %copy-done), custom_call_target="tpu_custom_call" | custom-call | tf_op jit(solution)/shard_map/pallas_call | solution.py:41
  20.5 4.4 %collective-permute-start.6 = (bf16[7,2,8,3360]{3,2,1,0:T(8,128)(2,1)S(1)}, bf16[7,2,8,3360]{3,2,1,0:T(8,128)(2,1)}, u32[]{:S(2)}, u32[]{:S(2)}) collective-permute-start(bf16[7,2,8,3360]{3,2,1,0:T(8,128)(2,1)S(1)} %shard_map.82.s1.mine_a), channel_id=1, source_target_pairs={{0,4},{4,8},{8,12},{1,5},{5,9},{9,13},{2,6},{6,10},{10,14},{3,7},{... | collective-permute-start | bytes 2257928 | tf_op jit(solution)/shard_map/ppermute | solution.py:20
  24.9 0.0 collective-permute-done.1
  24.9 2.0 %collective-permute-start.2 = (bf16[40,640]{1,0:T(8,128)(2,1)S(1)}, bf16[40,640]{1,0:T(8,128)(2,1)S(1)}, u32[]{:S(2)}, u32[]{:S(2)}) collective-permute-start(bf16[40,640]{1,0:T(8,128)(2,1)S(1)} %fusion), channel_id=1, source_target_pairs={{0,8},{4,12},{1,9},{5,13},{2,10},{6,14},{3,11},{7,15},{16,24},{20,... | collective-permute-start | bytes 153608 | tf_op jit(solution)/shard_map/ppermute | solution.py:20
  26.9 3.5 %collective-permute-start.7 = (bf16[4,2,8,3360]{3,2,1,0:T(8,128)(2,1)}, bf16[4,2,8,3360]{3,2,1,0:T(8,128)(2,1)}, u32[]{:S(2)}, u32[]{:S(2)}) collective-permute-start(bf16[4,2,8,3360]{3,2,1,0:T(8,128)(2,1)} %get-tuple-element.5.mine_b), channel_id=1, source_target_pairs={{0,4},{4,8},{8,12},{1,5},{5,9},{9,13},{2,6},{6,10},{10,14},{3,7},{... | collective-permute-start | bytes 1290248 | tf_op jit(solution)/shard_map/ppermute | solution.py:20
  30.4 12.3 %collective-permute-done.2 = bf16[40,640]{1,0:T(8,128)(2,1)S(1)} collective-permute-done((bf16[40,640]{1,0:T(8,128)(2,1)S(1)}, bf16[40,640]{1,0:T(8,128)(2,1)S(1)}, u32[]{:S(2)}, u32[]{:S(2)}) %collective-permute-start.2) | collective-permute-done | bytes 51232 | tf_op jit(solution)/shard_map/ppermute | solution.py:20
  42.7 0.7 %bitcast_dynamic-update-slice_fusion.1 = (f32[2,40,640]{2,1,0:T(8,128)S(1)}, f32[40,640]{1,0:T(8,128)}) fusion(f32[2,40,640]{2,1,0:T(8,128)S(1)} %shard_map.77.state, s32[]{:T(128)S(6)} %select_n.19, bf16[40,640]{1,0:T(8,128)(2,1)S(1)} %collective-permute-done.2, f32[40,640]{1,0:T(8,128)S(1)} %get-tuple-element.4, bf16[40,640]{1,0:T(8,128)(2,1)S(1)} %collective-permute-done.1), kind=kLoop, calls=%fused_computation.3 | loop fusion | flops 102400 | bytes 409604 | tf_op jit(solution)/shard_map/jit(dynamic_update_index_in_dim)/dynamic_update_slice | solution.py:423
  43.4 1.5 %collective-permute-start.3 = (f32[40,640]{1,0:T(8,128)}, f32[40,640]{1,0:T(8,128)}, u32[]{:S(2)}, u32[]{:S(2)}) collective-permute-start(f32[40,640]{1,0:T(8,128)} %get-tuple-element.7), channel_id=1, source_target_pairs={{0,2},{2,0},{1,3},{3,1},{4,6},{6,4},{5,7},{7,5},{8,10},{10,8},{9,1... | collective-permute-start | bytes 307208 | tf_op jit(solution)/shard_map/ppermute | solution.py:20
  44.8 1.0 %shard_map.81.s0.mine_s0 = bf16[5,2,8,3360]{3,2,1,0:T(8,128)(2,1)S(1)} custom-call(bf16[2,8,2,8,3360]{4,3,2,1,0:T(8,128)(2,1)S(1)} %bitcast.22, f32[3,3,2,3360]{3,2,1,0:T(2,128)S(1)} %copy-done), custom_call_target="tpu_custom_call" | custom-call | tf_op jit(solution)/shard_map/pallas_call | solution.py:41
  45.9 0.0 collective-permute-done.4.raw
  45.9 0.0 copy-start.1
  45.9 0.9 %copy-done.1 = f32[3,2,3360]{2,1,0:T(2,128)S(1)} copy-done((f32[3,2,3360]{2,1,0:T(2,128)S(1)}, f32[3,2,3360]{2,1,0:T(2,128)}, u32[]{:S(2)}) %copy-start.1) | copy-done | bytes 80664
  46.8 2.9 %shard_map.83 = bf16[5,8,3360]{2,1,0:T(8,128)(2,1)S(1)} custom-call(bf16[7,2,8,3360]{3,2,1,0:T(8,128)(2,1)} %collective-permute-done.4.raw, bf16[5,2,8,3360]{3,2,1,0:T(8,128)(2,1)S(1)} %shard_map.81.s0.mine_s0, bf16[7,2,8,3360]{3,2,1,0:T(8,128)(2,1)S(1)} %shard_map.82.s1.mine_a, f32[3,3,2,3360]{3,2,1,0:T(2,128)S(1)} %copy-done, f32[3,2,3360]{2,1,0:T(2,128)S(1)} %copy-done.1), custom_call_target="tpu_custom_call" | custom-call | tf_op jit(solution)/shard_map/pallas_call | solution.py:41
  49.7 4.6 %collective-permute-start.5 = (bf16[5,8,3360]{2,1,0:T(8,128)(2,1)S(1)}, bf16[5,8,3360]{2,1,0:T(8,128)(2,1)S(1)}, u32[]{:S(2)}, u32[]{:S(2)}) collective-permute-start(bf16[5,8,3360]{2,1,0:T(8,128)(2,1)S(1)} %shard_map.83), channel_id=1, source_target_pairs={{0,4},{4,8},{8,12},{1,5},{5,9},{9,13},{2,6},{6,10},{10,14},{3,7},{... | collective-permute-start | bytes 806408 | tf_op jit(solution)/shard_map/ppermute | solution.py:20
  54.4 0.0 collective-permute-done.3
  54.4 0.9 %bitcast_dynamic-update-slice_fusion.state = f32[2,40,640]{2,1,0:T(8,128)S(1)} fusion(f32[2,40,640]{2,1,0:T(8,128)S(1)} %get-tuple-element.6, s32[]{:T(128)S(6)} %select_n.21, f32[40,640]{1,0:T(8,128)} %collective-permute-done.3), kind=kLoop, calls=%fused_computation.2 | loop fusion | bytes 204804 | tf_op jit(solution)/shard_map/jit(dynamic_update_index_in_dim)/dynamic_update_slice | solution.py:425
  55.3 1.4 %shard_map.80 = bf16[128,1120]{1,0:T(8,128)(2,1)} custom-call(bf16[128,1120]{1,0:T(8,128)(2,1)S(1)} %bitcast.25, f32[2,40,640]{2,1,0:T(8,128)S(1)} %bitcast_dynamic-update-slice_fusion.state), custom_call_target="tpu_custom_call" | custom-call | tf_op jit(solution)/shard_map/pallas_call | solution.py:41
  56.7 0.0 collective-permute-done.7.before_b
  56.7 0.0 collective-permute-done.6.before_a
  56.7 4.3 %shard_map.84.gated = bf16[2,8,8,3360]{3,2,1,0:T(8,128)(2,1)} custom-call(s32[4]{0:T(128)S(1)} %pad_add_fusion.info, bf16[7,2,8,3360]{3,2,1,0:T(8,128)(2,1)S(1)} %shard_map.82.s1.mine_a, bf16[4,2,8,3360]{3,2,1,0:T(8,128)(2,1)} %get-tuple-element.5.mine_b, bf16[5,2,8,3360]{3,2,1,0:T(8,128)(2,1)S(1)} %shard_map.81.s0.mine_s0, ...), custom_call_target="tpu_custom_call" | custom-call | tf_op jit(solution)/shard_map/pallas_call | solution.py:41
  61.0 0.6 shard_map.85
  (13 shorter events, 0.0 us)
Async XLA Ops:
  0.6 1.7 %copy-start.3 = (bf16[2,8,8,1120]{3,2,1,0:T(8,128)(2,1)S(1)}, bf16[2,8,8,1120]{3,2,1,0:T(8,128)(2,1)}, u32[]{:S(2)}) copy-start(bf16[2,8,8,1120]{3,2,1,0:T(8,128)(2,1)} %param.7) | copy-start | bytes 860164
  0.7 1.7 %copy-start.4 = (bf16[2,8,8,1120]{3,2,1,0:T(8,128)(2,1)S(1)}, bf16[2,8,8,1120]{3,2,1,0:T(8,128)(2,1)}, u32[]{:S(2)}) copy-start(bf16[2,8,8,1120]{3,2,1,0:T(8,128)(2,1)} %param.8) | copy-start | bytes 860164
  2.8 10.3 %copy-start = (f32[3,3,2,3360]{3,2,1,0:T(2,128)S(1)}, f32[3,3,2,3360]{3,2,1,0:T(2,128)}, u32[]{:S(2)}) copy-start(f32[3,3,2,3360]{3,2,1,0:T(2,128)} %weight.7) | copy-start | bytes 725764
  3.4 9.6 %collective-permute-start = (bf16[5,8,3360]{2,1,0:T(8,128)(2,1)S(1)}, bf16[5,8,3360]{2,1,0:T(8,128)(2,1)S(1)}, u32[]{:S(2)}, u32[]{:S(2)}) collective-permute-start(bf16[5,8,3360]{2,1,0:T(8,128)(2,1)S(1)} %shard_map.78), channel_id=1, source_target_pairs={{0,2},{2,0},{1,3},{3,1},{4,6},{6,4},{5,7},{7,5},{8,10},{10,8},{9,1... | collective-permute-start | bytes 806408 | tf_op jit(solution)/shard_map/ppermute | solution.py:20
  7.4 38.5 %collective-permute-start.4 = (bf16[7,2,8,3360]{3,2,1,0:T(8,128)(2,1)}, bf16[7,2,8,3360]{3,2,1,0:T(8,128)(2,1)}, u32[]{:S(2)}, u32[]{:S(2)}) collective-permute-start(bf16[7,2,8,3360]{3,2,1,0:T(8,128)(2,1)} %slice_bitcast_fusion), channel_id=1, source_target_pairs={{4,0},{8,4},{12,8},{5,1},{9,5},{13,9},{6,2},{10,6},{14,10},{7,3},{... | collective-permute-start | bytes 2257928 | tf_op jit(solution)/shard_map/ppermute | solution.py:20
  15.4 9.5 %collective-permute-start.1 = (bf16[40,640]{1,0:T(8,128)(2,1)S(1)}, bf16[40,640]{1,0:T(8,128)(2,1)S(1)}, u32[]{:S(2)}, u32[]{:S(2)}) collective-permute-start(bf16[40,640]{1,0:T(8,128)(2,1)S(1)} %convert_element_type.15), channel_id=1, source_target_pairs={{0,4},{4,8},{8,12},{1,5},{5,9},{9,13},{2,6},{6,10},{10,14},{3,7},{... | collective-permute-start | bytes 153608 | tf_op jit(solution)/shard_map/ppermute | solution.py:20
  20.5 36.2 %collective-permute-start.6 = (bf16[7,2,8,3360]{3,2,1,0:T(8,128)(2,1)S(1)}, bf16[7,2,8,3360]{3,2,1,0:T(8,128)(2,1)}, u32[]{:S(2)}, u32[]{:S(2)}) collective-permute-start(bf16[7,2,8,3360]{3,2,1,0:T(8,128)(2,1)S(1)} %shard_map.82.s1.mine_a), channel_id=1, source_target_pairs={{0,4},{4,8},{8,12},{1,5},{5,9},{9,13},{2,6},{6,10},{10,14},{3,7},{... | collective-permute-start | bytes 2257928 | tf_op jit(solution)/shard_map/ppermute | solution.py:20
  24.9 17.8 %collective-permute-start.2 = (bf16[40,640]{1,0:T(8,128)(2,1)S(1)}, bf16[40,640]{1,0:T(8,128)(2,1)S(1)}, u32[]{:S(2)}, u32[]{:S(2)}) collective-permute-start(bf16[40,640]{1,0:T(8,128)(2,1)S(1)} %fusion), channel_id=1, source_target_pairs={{0,8},{4,12},{1,9},{5,13},{2,10},{6,14},{3,11},{7,15},{16,24},{20,... | collective-permute-start | bytes 153608 | tf_op jit(solution)/shard_map/ppermute | solution.py:20
  26.9 29.8 %collective-permute-start.7 = (bf16[4,2,8,3360]{3,2,1,0:T(8,128)(2,1)}, bf16[4,2,8,3360]{3,2,1,0:T(8,128)(2,1)}, u32[]{:S(2)}, u32[]{:S(2)}) collective-permute-start(bf16[4,2,8,3360]{3,2,1,0:T(8,128)(2,1)} %get-tuple-element.5.mine_b), channel_id=1, source_target_pairs={{0,4},{4,8},{8,12},{1,5},{5,9},{9,13},{2,6},{6,10},{10,14},{3,7},{... | collective-permute-start | bytes 1290248 | tf_op jit(solution)/shard_map/ppermute | solution.py:20
  43.4 11.0 %collective-permute-start.3 = (f32[40,640]{1,0:T(8,128)}, f32[40,640]{1,0:T(8,128)}, u32[]{:S(2)}, u32[]{:S(2)}) collective-permute-start(f32[40,640]{1,0:T(8,128)} %get-tuple-element.7), channel_id=1, source_target_pairs={{0,2},{2,0},{1,3},{3,1},{4,6},{6,4},{5,7},{7,5},{8,10},{10,8},{9,1... | collective-permute-start | bytes 307208 | tf_op jit(solution)/shard_map/ppermute | solution.py:20
  45.9 0.9 %copy-start.1 = (f32[3,2,3360]{2,1,0:T(2,128)S(1)}, f32[3,2,3360]{2,1,0:T(2,128)}, u32[]{:S(2)}) copy-start(f32[3,2,3360]{2,1,0:T(2,128)} %temporal.3) | copy-start | bytes 241924
  46.8 8.5 %copy-start.5 = (bf16[2,8,8,1120]{3,2,1,0:T(8,128)(2,1)S(1)}, bf16[2,8,8,1120]{3,2,1,0:T(8,128)(2,1)}, u32[]{:S(2)}) copy-start(bf16[2,8,8,1120]{3,2,1,0:T(8,128)(2,1)} %param.6) | copy-start | bytes 860164
  46.8 9.9 %copy-start.2 = (f32[3,2,3360]{2,1,0:T(2,128)S(1)}, f32[3,2,3360]{2,1,0:T(2,128)}, u32[]{:S(2)}) copy-start(f32[3,2,3360]{2,1,0:T(2,128)} %temporal.3) | copy-start | bytes 241924
  49.7 11.3 %collective-permute-start.5 = (bf16[5,8,3360]{2,1,0:T(8,128)(2,1)S(1)}, bf16[5,8,3360]{2,1,0:T(8,128)(2,1)S(1)}, u32[]{:S(2)}, u32[]{:S(2)}) collective-permute-start(bf16[5,8,3360]{2,1,0:T(8,128)(2,1)S(1)} %shard_map.83), channel_id=1, source_target_pairs={{0,4},{4,8},{8,12},{1,5},{5,9},{9,13},{2,6},{6,10},{10,14},{3,7},{... | collective-permute-start | bytes 806408 | tf_op jit(solution)/shard_map/ppermute | solution.py:20

commit v3 on v2

v3 whole, which is shorter than its diff:
```python
import functools

import jax
import jax.numpy as jnp
from jax import lax
from jax.experimental import pallas as pl
from jax.experimental.pallas import tpu as pltpu
from jax.sharding import PartitionSpec as P


HEAD_DIM = 32
LANES = 128
STATE_ROWS = HEAD_DIM + 8
BLOCK = 8
TOP, BOTTOM, SPACE, SPAN, EVEN = range(5)
F32 = jnp.float32
BF16 = jnp.bfloat16


def counter_ring(value, upward):
    groups, count = (lax.axis_size("groups"), lax.axis_size("tm"))
    pairs = []
    for group in range(groups):
        other = group ^ 1
        ahead = 1 if (group % 2 == 0) == upward else -1
        for at in range(count):
            target = (group, at + ahead)
            if not 0 <= at + ahead < count:
                target = (other, at) if other < groups else (group, (at + ahead) % count)
            pairs.append((group * count + at, target[0] * count + target[1]))
    return lax.ppermute(value, ("groups", "tm"), pairs)


def rotated(value, axis, steps):
    count = lax.axis_size(axis)
    return lax.ppermute(value, axis, [(source, (source + steps) % count) for source in range(count)])


VMEM = pl.BlockSpec(memory_space=pltpu.VMEM)
SMEM = pl.BlockSpec(memory_space=pltpu.SMEM)
ANY = pl.BlockSpec(memory_space=pl.ANY)


def kernel_call(kernel, out_shape, operands, specs=None, out_specs=None, scratch=(), aliases=None, vmem_mib=16):
    many = isinstance(out_shape, tuple)
    return pl.pallas_call(
        kernel,
        out_shape=out_shape,
        in_specs=[VMEM] * len(operands) if specs is None else specs,
        out_specs=out_specs if out_specs is not None else ((VMEM,) * len(out_shape) if many else VMEM),
        scratch_shapes=scratch,
        input_output_aliases=aliases or {},
        compiler_params=pltpu.CompilerParams(vmem_limit_bytes=vmem_mib << 20),
    )(*operands)


def lane_tiles(channels, body):
    full = channels // LANES

    @pl.loop(0, full)
    def _(tile):
        body(pl.ds(pl.multiple_of(tile * LANES, LANES), LANES), LANES)

    if channels % LANES:
        body(pl.ds(full * LANES, channels % LANES), channels % LANES)


def spread(row, columns, width):
    return jnp.broadcast_to(row, (columns, width))


def tap_weights(weight_ref, part, lanes, width, columns):
    column = lax.broadcasted_iota(jnp.int32, (columns, width), 0)
    taps = []
    for row_tap in range(3):
        row = []
        for col_tap in range(3):
            w = spread(weight_ref[row_tap, col_tap, part : part + 1, lanes], columns, width)
            if col_tap == 0:
                w = jnp.where(column == columns - 1, 0.0, w)
            if col_tap == 2:
                w = jnp.where(column == 0, 0.0, w)
            row.append(w)
        taps.append(row)
    return taps


def conv_row(above, here, below, taps, columns):
    sums = [taps[0][b] * above + taps[1][b] * here + taps[2][b] * below for b in range(3)]
    total = sums[1] + pltpu.roll(sums[0], 1, 0) + pltpu.roll(sums[2], columns - 1, 0)
    return total.astype(BF16)


def conv_interior(load, wanted, taps, columns):
    held = {}

    def row(r):
        if r not in held:
            held[r] = load(r)
        return held[r]

    return [conv_row(row(r - 1), row(r), row(r + 1), taps, columns) for r in wanted]


def either(flag, body, first, second):
    @pl.when(flag)
    def _():
        body(first, second)

    @pl.when(jnp.logical_not(flag))
    def _():
        body(second, first)


def conv_a_kernel(info, frames, weight, first, second):
    columns, channels = frames.shape[3:]
    count = first.shape[0]

    def body(out, raw):
        def tile(lanes, width):
            for part in range(2):
                taps = tap_weights(weight, part, lanes, width, columns)
                for r in range(count):
                    raw[r, part, :, lanes] = frames[0, r, part, :, lanes]

                def load(r, part=part):
                    return frames[1, r, part, :, lanes].astype(F32)

                for at, value in enumerate(conv_interior(load, range(1, count + 1), taps, columns)):
                    out[at, part, :, lanes] = value

        lane_tiles(channels, tile)

    either(info[EVEN] == 1, body, first, second)


def conv_s0_kernel(wanted, frames, weight, out):
    columns, channels = frames.shape[3:]

    def tile(lanes, width):
        for part in range(2):
            taps = tap_weights(weight, part, lanes, width, columns)

            def load(r, part=part):
                return frames[0, r, part, :, lanes].astype(F32)

            for at, value in enumerate(conv_interior(load, wanted, taps, columns)):
                out[at, part, :, lanes] = value

    lane_tiles(channels, tile)


def slab_places(chunk, channels):
    per_slab = channels // chunk
    return [(block // per_slab, block % per_slab * chunk) for block in range(STATE_ROWS // BLOCK)]


def pack_kernel(edges, step, info, frames, state, out):
    row_count, _, columns, channels = frames.shape[1:]
    chunks, _, chunk = state.shape
    index = lax.rem(info[SPACE] + step, chunks)
    at = 0
    if edges is not None:
        row = {
            "either": jnp.where(info[SPACE] == 0, row_count - 1, 0),
            "head": 0,
            "tail": row_count - 1,
        }[edges]
        for frame in range(2):
            for part in range(2):
                out[at] = frames[frame, row, part]
                at += 1
    places = slab_places(chunk, channels)
    for slab in range(places[-1][0] + 1):
        out[at + slab] = jnp.zeros((columns, channels), BF16)
    for block, (slab, lane) in enumerate(places):
        out[at + slab, :, lane : lane + chunk] = state[
            index, block * BLOCK : (block + 1) * BLOCK, :
        ].astype(BF16)


def boundary_kernel(n_packs, first_of, top_at, bottom_at, info, frames, weight, state, *refs):
    packs, (out, first, second, total, rounded) = (refs[:n_packs], refs[n_packs:])
    row_count, _, columns, channels = frames.shape[1:]
    has_top, has_bottom = (info[TOP].astype(F32), info[BOTTOM].astype(F32))
    chunk = state.shape[2]
    joined = first.shape[0] - 2

    def body(spatial, raw):
        def tile(lanes, width):
            for part in range(2):
                taps = tap_weights(weight, part, lanes, width, columns)
                for i in range(2):
                    raw[i, part, :, lanes] = frames[0, row_count - 2 + i, part, :, lanes]
                for i in range(joined):
                    raw[2 + i, part, :, lanes] = jnp.zeros((columns, width), BF16)
                for frame in range(2):

                    def load(r, frame=frame, part=part):
                        if r < 0:
                            return packs[top_at][2 * frame + part, :, lanes].astype(F32) * has_top
                        if r == row_count:
                            return packs[bottom_at][2 * frame + part, :, lanes].astype(F32) * has_bottom
                        return frames[frame, r, part, :, lanes].astype(F32)

                    values = conv_interior(load, (0, row_count - 1), taps, columns)
                    for i, value in enumerate(values):
                        out[2 * frame + i, part, :, lanes] = value
                        if frame == 1:
                            spatial[i, part, :, lanes] = value
                    if frame == 0 and joined == 2:
                        for i, value in enumerate(values):
                            spatial[2 + i, part, :, lanes] = value

        lane_tiles(channels, tile)
        if joined == 1:
            spatial[2] = out[jnp.where(info[SPACE] == 0, 1, 0)]

    either(info[EVEN] == 1, body, first, second)
    for block, (slab, lane) in enumerate(slab_places(chunk, channels)):
        rows = slice(block * BLOCK, (block + 1) * BLOCK)
        value = state[info[SPACE], rows, :]
        for pack, begin in zip(packs, first_of):
            value = value + pack[begin + slab, :, lane : lane + chunk].astype(F32)
        total[rows, :] = value
        rounded[rows, :] = value.astype(BF16)


def scan_kernel(step, info, own, earlier, total, rounded):
    value = own[...] + jnp.where(info[SPAN] >= step, earlier[...].astype(F32), 0.0)
    total[...] = value
    rounded[...] = value.astype(BF16)


def gate(value, key):
    return value * (key / (1.0 + jnp.exp(-key)))


def theirs_kernel(wanted, edge, info, first, second, *refs):
    if edge is None:
        sent_first, sent_second, s0, weight, temporal, out = refs
    else:
        last_first, last_second, sent_first, sent_second, b, s0, weight, temporal, out = refs
    columns, channels = first.shape[2:]
    held_rows = first.shape[0]
    row_count = held_rows + 2

    def body(ahead, behind):
        raw, s1 = (behind[0], ahead[1])

        def tile(lanes, width):
            mixed = []
            for part in range(2):
                taps = tap_weights(weight, part, lanes, width, columns)
                w = [spread(temporal[tap, part : part + 1, lanes], columns, width) for tap in range(3)]
                held = {}

                def load(r, part=part, held=held):
                    if r not in held:
                        ref, at = (raw, r) if r < held_rows else (behind[2], r - held_rows)
                        held[r] = ref[at, part, :, lanes].astype(F32)
                    return held[r]

                values = conv_interior(load, wanted, taps, columns)
                rows = [
                    w[0] * s0[r - 1, part, :, lanes].astype(F32)
                    + w[1] * s1[r - 1, part, :, lanes].astype(F32)
                    + w[2] * value.astype(F32)
                    for r, value in zip(wanted, values)
                ]
                if edge:
                    at_start = info[SPACE] == 0
                    last = row_count - 1
                    value = conv_row(
                        jnp.where(at_start, 0.0, load(last - 1)),
                        jnp.where(at_start, load(0), load(last)),
                        jnp.where(at_start, load(1), 0.0),
                        taps,
                        columns,
                    )
                    at = jnp.where(at_start, 0, 1)
                    rows.append(
                        w[0] * b[at, part, :, lanes].astype(F32)
                        + w[1] * b[2 + at, part, :, lanes].astype(F32)
                        + w[2] * value.astype(F32)
                    )
                mixed.append(rows)
            for r in range(out.shape[0]):
                out[r, :, lanes] = gate(mixed[0][r], mixed[1][r]).astype(BF16)

        lane_tiles(channels, tile)

    pair = ((first, sent_first), (second, sent_second))
    if edge is not None:
        pair = (pair[0] + (last_first,), pair[1] + (last_second,))
    either(info[EVEN] == 1, body, *pair)


def ours_kernel(
    joined, info, first, second, b_first, b_second, sent_first, sent_second, mine_b, mine_s0, temporal, out, late, early, sems
):
    row_count, columns, channels = late.shape
    alive = jnp.where(info[SPAN] == 0, 0.0, 1.0)
    at_start = info[SPACE] == 0

    def weights(lanes, width):
        return [
            [spread(temporal[tap, part : part + 1, lanes], columns, width) for tap in range(3)]
            for part in range(2)
        ]

    def late_copy():
        return pltpu.make_async_copy(late, out.at[1], sems.at[0])

    def early_copy(at, row):
        return pltpu.make_async_copy(early.at[at], out.at[0, row], sems.at[1 + at])

    def body(ahead, behind):
        before_a, before_b, mine_a = (ahead[0], ahead[1], behind[2])

        def load(ref, at, part, lanes):
            return ref[at, part, :, lanes].astype(F32)

        def last_frame(lanes, width):
            w = weights(lanes, width)
            for r in range(row_count):
                edge, end = (r in (0, row_count - 1), int(r > 0))
                mixed = []
                for p in range(2):
                    before = load(before_b, end, p, lanes) if edge else load(before_a, r - 1, p, lanes)
                    s0 = load(mine_b, end, p, lanes) if edge else load(mine_s0, r - 1, p, lanes)
                    s1 = load(mine_b, 2 + end, p, lanes) if edge else load(mine_a, r - 1, p, lanes)
                    mixed.append((w[p][0] * alive) * before + w[p][1] * s0 + w[p][2] * s1)
                late[r, :, lanes] = gate(*mixed).astype(BF16)

        def joined_rows(lanes, width):
            w = weights(lanes, width)
            for i in range(joined):
                end = jnp.where(at_start, 1, 0) if joined == 1 else i
                mixed = [
                    (w[p][0] * alive) * load(before_b, 2 + i, p, lanes)
                    + (w[p][1] * alive) * load(before_b, end, p, lanes)
                    + w[p][2] * load(mine_b, end, p, lanes)
                    for p in range(2)
                ]
                early[i, :, lanes] = gate(*mixed).astype(BF16)

        lane_tiles(channels, last_frame)
        late_copy().start()
        lane_tiles(channels, joined_rows)

    either(
        info[EVEN] == 1,
        body,
        (first, b_first, sent_second),
        (second, b_second, sent_first),
    )
    if joined == 1:
        ends = [jnp.where(at_start, row_count - 1, 0)]
    else:
        ends = [0, row_count - 1]
    for i, row in enumerate(ends):
        early_copy(i, row).start()

    @pl.when(info[SPAN] == 0)
    def _():
        def made(lanes, width):
            w = weights(lanes, width)
            for r in range(row_count - 2):
                mixed = [w[p][2] * mine_s0[r, p, :, lanes].astype(F32) for p in range(2)]
                early[joined + r, :, lanes] = gate(*mixed).astype(BF16)
            if joined == 1:
                mixed = [w[p][2] * mine_b[jnp.where(at_start, 0, 1), p, :, lanes].astype(F32) for p in range(2)]
                early[joined + row_count - 2, :, lanes] = gate(*mixed).astype(BF16)

        lane_tiles(channels, made)
        rows = list(range(1, row_count - 1))
        if joined == 1:
            rows.append(jnp.where(at_start, 0, row_count - 1))
        for r, row in enumerate(rows):
            early_copy(joined + r, row).start()
        for r, row in enumerate(rows):
            early_copy(joined + r, row).wait()

    for i, row in enumerate(ends):
        early_copy(i, row).wait()
    late_copy().wait()


def place_kernel(joined, row_count, info, rows, more, gated, out, sems):
    @pl.when(info[SPAN] != 0)
    def _():
        copies = []
        for r in range(row_count - 2 + 2 - joined):
            source = rows.at[r] if r < rows.shape[0] else more.at[r - rows.shape[0]]
            target = r + 1 if r < row_count - 2 else jnp.where(info[SPACE] == 0, 0, row_count - 1)
            copies.append(pltpu.make_async_copy(source, out.at[0, target], sems.at[r]))
        for copy in copies:
            copy.start()
        for copy in copies:
            copy.wait()


def head_mask(width):
    row = lax.broadcasted_iota(jnp.int32, (width, width), 0) // HEAD_DIM
    column = lax.broadcasted_iota(jnp.int32, (width, width), 1) // HEAD_DIM
    return row == column


def lane_groups(channels):
    return [(at, min(LANES, channels - at)) for at in range(0, channels, LANES)]


def state_kernel(key, value, state):
    tokens, channels = key.shape
    chunk = state.shape[2]
    ones = jnp.ones((8, tokens), BF16)
    state[...] = jnp.zeros_like(state)
    for at, width in lane_groups(channels):
        keys = jnp.maximum(key[:, at : at + width], 0)
        product = lax.dot_general(
            keys, value[:, at : at + width], (((0,), (0,)), ((), ())), preferred_element_type=F32
        )
        product = jnp.where(head_mask(width), product, 0.0)
        folded = sum(product[d : d + HEAD_DIM] for d in range(0, width, HEAD_DIM))
        lanes = slice(at % chunk, at % chunk + width)
        state[at // chunk, :HEAD_DIM, lanes] = folded
        state[at // chunk, HEAD_DIM:, lanes] = jnp.dot(ones, keys, preferred_element_type=F32)


def split(value):
    high = value.astype(BF16)
    return (high, (value - high.astype(F32)).astype(BF16))


def attend_kernel(info, query, own, *refs):
    others, (out, held) = (refs[:-2], refs[-2:])
    channels = query.shape[1]
    chunks, _, chunk = held.shape
    held[info[SPACE]] = own[...]
    for step, other in enumerate(others):
        held[lax.rem(info[SPACE] + (chunks - 1 - step), chunks)] = other[...]
    for at, width in lane_groups(channels):
        rows = jnp.maximum(query[:, at : at + width], 0)
        lanes = slice(at % chunk, at % chunk + width)
        mask = head_mask(width)
        folded = held[at // chunk, :HEAD_DIM, lanes]
        kv = jnp.where(mask, jnp.concatenate([folded] * (width // HEAD_DIM), axis=0), 0.0)
        sums = jnp.where(
            mask, jnp.broadcast_to(held[at // chunk, HEAD_DIM : HEAD_DIM + 1, lanes], (width, width)), 0.0
        )
        numerator = sum(jnp.dot(rows, part, preferred_element_type=F32) for part in split(kv))
        denominator = sum(
            lax.dot_general(rows, part, (((1,), (1,)), ((), ())), preferred_element_type=F32)
            for part in split(sums)
        )
        out[:, at : at + width] = (numerator / (denominator + 1.0)).astype(BF16)


def local_state(key, value, chunks):
    channels = key.shape[1]
    groups = pl.cdiv(pl.cdiv(channels, LANES), chunks)
    return kernel_call(state_kernel, jax.ShapeDtypeStruct((chunks, STATE_ROWS, groups * LANES), F32), (key, value))


def layer(query_proj, key_proj, value_proj, expanded, spatial_weight, temporal_weight):
    frames, row_count, col_count, channels = query_proj.shape
    hidden = expanded.shape[4]
    assert frames == 2 and row_count >= 6
    space, spaces = (lax.axis_index("space"), lax.axis_size("space"))
    joined = 1 if spaces == 2 else 2
    interior = row_count - 2
    early_rows = interior - 2
    info = jnp.stack(
        [space > 0, space < spaces - 1, space, lax.axis_index("tm"), lax.axis_index("groups") % 2 == 0]
    ).astype(jnp.int32)

    def tokens(array):
        return array.reshape(-1, channels)

    def rows_of(count):
        return jax.ShapeDtypeStruct((count, 2, col_count, hidden), BF16)

    held = lax.optimization_barrier(jnp.transpose(expanded, (0, 1, 3, 2, 4)))
    sent_first, sent_second = kernel_call(
        conv_a_kernel, (rows_of(interior), rows_of(interior)), (info, held, spatial_weight), [SMEM, VMEM, VMEM]
    )
    first = counter_ring(sent_first, True)
    second = counter_ring(sent_second, False)

    state = local_state(tokens(key_proj), tokens(value_proj), spaces)
    chunk = state.shape[2]
    slabs = slab_places(chunk, hidden)[-1][0] + 1
    packs, first_of, top_at, bottom_at = ([], [], None, None)
    for step in range(1, spaces):
        edges = "either" if spaces == 2 else {1: "tail", spaces - 1: "head"}.get(step)
        edge_rows = 4 if edges else 0
        if edges in ("tail", "either"):
            top_at = step - 1
        if edges in ("head", "either"):
            bottom_at = step - 1
        packed = kernel_call(
            functools.partial(pack_kernel, edges, step),
            jax.ShapeDtypeStruct((edge_rows + slabs, col_count, hidden), BF16),
            (info, held, state),
            [SMEM, VMEM, VMEM],
        )
        packs.append(rotated(packed, "space", step))
        first_of.append(edge_rows)

    mine_s0 = kernel_call(
        functools.partial(conv_s0_kernel, tuple(range(1, row_count - 1))), rows_of(interior), (held, spatial_weight)
    )
    summed = (jax.ShapeDtypeStruct((STATE_ROWS, chunk), F32), jax.ShapeDtypeStruct((STATE_ROWS, chunk), BF16))
    mine_b, b_sent_first, b_sent_second, own, rounded = kernel_call(
        functools.partial(boundary_kernel, len(packs), tuple(first_of), top_at, bottom_at),
        (rows_of(4), rows_of(2 + joined), rows_of(2 + joined)) + summed,
        (info, held, spatial_weight, state, *packs),
        [SMEM] + [VMEM] * (3 + len(packs)),
    )
    step = 1
    while step < lax.axis_size("tm"):
        earlier = rotated(rounded, "tm", step)
        own, rounded = kernel_call(
            functools.partial(scan_kernel, step), summed, (info, own, earlier), [SMEM, VMEM, VMEM]
        )
        step *= 2
    b_first = counter_ring(b_sent_first, True)
    b_second = counter_ring(b_sent_second, False)

    theirs_early = kernel_call(
        functools.partial(theirs_kernel, tuple(range(1, early_rows + 1)), None),
        jax.ShapeDtypeStruct((early_rows, col_count, hidden), BF16),
        (info, first, second, sent_first, sent_second, mine_s0, spatial_weight, temporal_weight),
        [SMEM] + [VMEM] * 7,
    )
    back_early = rotated(theirs_early, "tm", 1)
    late_rows = tuple(range(early_rows + 1, interior + 1))
    theirs_late = kernel_call(
        functools.partial(theirs_kernel, late_rows, joined == 1),
        jax.ShapeDtypeStruct((len(late_rows) + 2 - joined, col_count, hidden), BF16),
        (
            info, first, second, b_first, b_second, sent_first, sent_second, mine_b, mine_s0,
            spatial_weight, temporal_weight,
        ),
        [SMEM] + [VMEM] * 10,
    )
    back_late = rotated(theirs_late, "tm", 1)

    others = [rotated(own, "space", step) for step in range(1, spaces)]
    attended = kernel_call(
        attend_kernel,
        jax.ShapeDtypeStruct((query_proj.size // channels, channels), BF16),
        (info, tokens(query_proj), own, *others),
        [SMEM] + [VMEM] * (2 + len(others)),
        scratch=[pltpu.VMEM((spaces, STATE_ROWS, chunk), F32)],
    ).reshape(query_proj.shape)

    gated_shape = jax.ShapeDtypeStruct((2, row_count, col_count, hidden), BF16)
    gated = kernel_call(
        functools.partial(ours_kernel, joined),
        gated_shape,
        (info, first, second, b_first, b_second, sent_first, sent_second, mine_b, mine_s0, temporal_weight),
        [SMEM] + [VMEM] * 9,
        ANY,
        [
            pltpu.VMEM(gated_shape.shape[1:], BF16),
            pltpu.VMEM(gated_shape.shape[1:], BF16),
            pltpu.SemaphoreType.DMA((1 + row_count,)),
        ],
    )
    gated = kernel_call(
        functools.partial(place_kernel, joined, row_count),
        gated_shape,
        (info, back_early, back_late, gated),
        [SMEM, VMEM, VMEM, ANY],
        ANY,
        [pltpu.SemaphoreType.DMA((row_count,))],
        {3: 0},
    )
    return (attended, gated)


def solution(mesh):
    return jax.shard_map(
        layer,
        mesh=mesh,
        in_specs=(
            P(("groups", "tm"), "space", None, "mp"),
            P(("groups", "tm"), "space", None, "mp"),
            P(("groups", "tm"), "space", None, "mp"),
            P(("groups", "tm"), "space", None, None, "mp"),
            P(None, None, None, "mp"),
            P(None, None, "mp"),
        ),
        out_specs=(
            P(("groups", "tm"), "space", None, "mp"),
            P(("groups", "tm"), "space", None, "mp"),
        ),
        check_vma=False,
    )
```

time: 62 us -> 58.2 us (0.939)
  starting transfers between devices: 24 us -> 14 us
  waiting for transfers between devices: 16.6 us -> 24 us
  Pallas kernels: 14.8 us -> 17.5 us
  local copies, waits for them, and re-layouts: 4.45 us -> 1.81 us
  other arithmetic: 0.84 us -> 0 us
    ppermute x8 -> x10, starting transfers between devices: 24 us -> 14 us  [the longest x6 8.79 us: rotated(): lax.ppermute(value, axis, [(source, (source + steps) % count) for source...]
    ppermute x8 -> x10, waiting for transfers between devices: 16.6 us -> 24 us  [the longest x6 19.7 us: rotated(): lax.ppermute(value, axis, [(source, (source + steps) % count) for source...]
    pallas_call x9 -> x12, Pallas kernels: 14.8 us -> 17.5 us  [kernel_call(): pl.pallas_call(kernel, out_shape=out_shape, in_specs=[VMEM] * len(operand...]
    squeeze x1 -> x0, local copies, waits for them, and re-layouts: 0.93 us -> none  [layer(): after = shifted(held[0, :sent + 2], 'tm', -1)]
    dynamic_update_slice x1 -> x0, local copies, waits for them, and re-layouts: 0.91 us -> none  [layer(): lax.dynamic_update_index_in_dim(whole, rotated(own, 'space', step), (spac...]
    unnamed x13 -> x11, local copies, waits for them, and re-layouts: 2.61 us -> 1.72 us
    dynamic_update_slice x1 -> x0, other arithmetic: 0.66 us -> none  [layer(): whole = lax.dynamic_update_index_in_dim(state, own, space, 0)]
  transfers between devices with their start and end apart: 8 -> 10, of which waited for: 2 -> 7; matrix products, arithmetic and copies ran while one was open for 4% -> 0% of each run, Pallas kernels for 22% -> 26%
where the time goes in v3:
time: 58.2 us; the launch traced here: 58.1 us
  waiting for transfers between devices  24 us (41%)
  Pallas kernels  17.5 us (30%)
  starting transfers between devices  14 us (24%)
  local copies, waits for them, and re-layouts  1.81 us (3%)
  between operations  0.78 us (1%)
    ppermute x6, waiting for transfers between devices, rotated(): lax.ppermute(value, axis, [(source, (source + steps) % count) for source...  19.7 us
    pallas_call x12, Pallas kernels, kernel_call(): pl.pallas_call(kernel, out_shape=out_shape, in_specs=[VMEM] * len(operand...  17.5 us
    ppermute x6, starting transfers between devices, rotated(): lax.ppermute(value, axis, [(source, (source + steps) % count) for source...  8.79 us
    ppermute x4, starting transfers between devices, counter_ring(): return lax.ppermute(value, ('groups', 'tm'), pairs)  5.19 us
    ppermute x4, waiting for transfers between devices, counter_ring(): return lax.ppermute(value, ('groups', 'tm'), pairs)  4.33 us
    unnamed x11, local copies, waits for them, and re-layouts  1.72 us
  transfers between devices with their start and end apart: 10, of which 7 were waited for; matrix products, arithmetic and copies ran while one was open for 0% of the time, Pallas kernels for 26%

profile of v3, /device:TPU:0, one launch (start us, length us, event | category | flops | bytes accessed | tf_op | source)
XLA Modules:
  0.0 58.1 jit_solution(13072723635532840612)
XLA Ops:
  0.7 1.7 %copy.11 = bf16[2,8,8,2,3360]{4,2,3,1,0:T(8,128)(2,1)S(1)} copy(bf16[2,8,8,2,3360]{4,3,2,1,0:T(2,128)(2,1)} %param.9) | data formatting | bytes 3440640 | tf_op args[3]
  2.4 0.1 stack.35.info
  2.5 1.8 %shard_map.83 = (bf16[6,2,8,3360]{3,2,1,0:T(8,128)(2,1)S(1)}, bf16[6,2,8,3360]{3,2,1,0:T(8,128)(2,1)S(1)}) custom-call(s32[5]{0:T(128)S(1)} %stack.35.info, bf16[2,8,2,8,3360]{4,3,2,1,0:T(8,128)(2,1)S(1)} %bitcast.12, f32[3,3,2,3360]{3,2,1,0:T(2,128)S(1)} %copy-done), custom_call_target="tpu_custom_call" | custom-call | tf_op jit(solution)/shard_map/pallas_call | solution.py:46
  4.3 3.1 %collective-permute-start.4 = (bf16[6,2,8,3360]{3,2,1,0:T(8,128)(2,1)S(1)}, bf16[6,2,8,3360]{3,2,1,0:T(8,128)(2,1)S(1)}, u32[]{:S(2)}, u32[]{:S(2)}) collective-permute-start(bf16[6,2,8,3360]{3,2,1,0:T(8,128)(2,1)S(1)} %get-tuple-element.17.refs_0_.refs_2_.sent_first), channel_id=1, source_target_pairs={{0,4},{4,8},{8,12},{12,28},{16,0},{20,16},{24,20},{28,24},{1,5},{5... | collective-permute-start | bytes 1935368 | tf_op jit(solution)/shard_map/ppermute | solution.py:31
  7.4 0.0 collective-permute-start.5
  7.4 0.3 shard_map.77.state
  7.7 0.6 shard_map.78
  8.3 2.0 %collective-permute-start = (bf16[5,8,3360]{2,1,0:T(8,128)(2,1)S(1)}, bf16[5,8,3360]{2,1,0:T(8,128)(2,1)S(1)}, u32[]{:S(2)}, u32[]{:S(2)}) collective-permute-start(bf16[5,8,3360]{2,1,0:T(8,128)(2,1)S(1)} %shard_map.78), channel_id=1, source_target_pairs={{0,2},{2,0},{1,3},{3,1},{4,6},{6,4},{5,7},{7,5},{8,10},{10,8},{9,1... | collective-permute-start | bytes 806408 | tf_op jit(solution)/shard_map/ppermute | solution.py:36
  10.3 6.1 %collective-permute-done.refs_0_ = bf16[5,8,3360]{2,1,0:T(8,128)(2,1)S(1)} collective-permute-done((bf16[5,8,3360]{2,1,0:T(8,128)(2,1)S(1)}, bf16[5,8,3360]{2,1,0:T(8,128)(2,1)S(1)}, u32[]{:S(2)}, u32[]{:S(2)}) %collective-permute-start) | collective-permute-done | bytes 268832 | tf_op jit(solution)/shard_map/ppermute | solution.py:36
  16.4 1.5 %shard_map.79 = (bf16[4,2,8,3360]{3,2,1,0:T(8,128)(2,1)S(1)}, bf16[3,2,8,3360]{3,2,1,0:T(8,128)(2,1)S(1)}, bf16[3,2,8,3360]{3,2,1,0:T(8,128)(2,1)S(1)}, f32[40,640]{1,0:T(8,128)S(1)}, bf16[40,640]{1,0:T(8,128)(2,1)S(1)}) custom-call(s32[5]{0:T(128)S(1)} %stack.35.info, bf16[2,8,2,8,3360]{4,3,2,1,0:T(8,128)(2,1)S(1)} %bitcast.14, ...), custom_call_target="tpu_custom_call" | custom-call | tf_op jit(solution)/shard_map/pallas_call | solution.py:46
  18.0 0.0 copy-start.1
  18.0 1.8 %collective-permute-start.7 = (bf16[3,2,8,3360]{3,2,1,0:T(8,128)(2,1)S(1)}, bf16[3,2,8,3360]{3,2,1,0:T(8,128)(2,1)S(1)}, u32[]{:S(2)}, u32[]{:S(2)}) collective-permute-start(bf16[3,2,8,3360]{3,2,1,0:T(8,128)(2,1)S(1)} %get-tuple-element.19), channel_id=1, source_target_pairs={{0,4},{4,8},{8,12},{12,28},{16,0},{20,16},{24,20},{28,24},{1,5},{5... | collective-permute-start | bytes 967688 | tf_op jit(solution)/shard_map/ppermute | solution.py:31
  19.8 0.3 collective-permute-start.8
  20.1 1.2 %shard_map.84.refs_2_.refs_5_.mine_s0 = bf16[6,2,8,3360]{3,2,1,0:T(8,128)(2,1)S(1)} custom-call(bf16[2,8,2,8,3360]{4,3,2,1,0:T(8,128)(2,1)S(1)} %bitcast.15, f32[3,3,2,3360]{3,2,1,0:T(2,128)S(1)} %copy-done), custom_call_target="tpu_custom_call" | custom-call | tf_op jit(solution)/shard_map/pallas_call | solution.py:46
  21.2 1.8 %collective-permute-done.4.first = bf16[6,2,8,3360]{3,2,1,0:T(8,128)(2,1)S(1)} collective-permute-done((bf16[6,2,8,3360]{3,2,1,0:T(8,128)(2,1)S(1)}, bf16[6,2,8,3360]{3,2,1,0:T(8,128)(2,1)S(1)}, u32[]{:S(2)}, u32[]{:S(2)}) %collective-permute-start.4) | collective-permute-done | bytes 645152 | tf_op jit(solution)/shard_map/ppermute | solution.py:31
  23.1 2.1 %collective-permute-done.5.second = bf16[6,2,8,3360]{3,2,1,0:T(8,128)(2,1)S(1)} collective-permute-done((bf16[6,2,8,3360]{3,2,1,0:T(8,128)(2,1)S(1)}, bf16[6,2,8,3360]{3,2,1,0:T(8,128)(2,1)S(1)}, u32[]{:S(2)}, u32[]{:S(2)}) %collective-permute-start.5) | collective-permute-done | bytes 645152 | tf_op jit(solution)/shard_map/ppermute | solution.py:31
  25.2 2.1 %shard_map.85 = bf16[4,8,3360]{2,1,0:T(8,128)(2,1)S(1)} custom-call(s32[5]{0:T(128)S(1)} %stack.35.info, bf16[6,2,8,3360]{3,2,1,0:T(8,128)(2,1)S(1)} %collective-permute-done.4.first, bf16[6,2,8,3360]{3,2,1,0:T(8,128)(2,1)S(1)} %collective-permute-done.5.second, bf16[6,2,8,3360]{3,2,1,0:T(8,128)(2,1)S(1)} %get-tuple-element.17.refs_0_.refs_2_.sent_first, ...), custom_call_target="tpu_custom_call" | custom-call | tf_op jit(solution)/shard_map/pallas_call | solution.py:46
  27.2 1.6 %collective-permute-start.6 = (bf16[4,8,3360]{2,1,0:T(8,128)(2,1)S(1)}, bf16[4,8,3360]{2,1,0:T(8,128)(2,1)S(1)}, u32[]{:S(2)}, u32[]{:S(2)}) collective-permute-start(bf16[4,8,3360]{2,1,0:T(8,128)(2,1)S(1)} %shard_map.85), channel_id=1, source_target_pairs={{0,4},{4,8},{8,12},{12,0},{1,5},{5,9},{9,13},{13,1},{2,6},{6,10},{... | collective-permute-start | bytes 645128 | tf_op jit(solution)/shard_map/ppermute | solution.py:36
  28.9 1.6 %collective-permute-start.1 = (bf16[40,640]{1,0:T(8,128)(2,1)S(1)}, bf16[40,640]{1,0:T(8,128)(2,1)S(1)}, u32[]{:S(2)}, u32[]{:S(2)}) collective-permute-start(bf16[40,640]{1,0:T(8,128)(2,1)S(1)} %get-tuple-element.13), channel_id=1, source_target_pairs={{0,4},{4,8},{8,12},{12,0},{1,5},{5,9},{9,13},{13,1},{2,6},{6,10},{... | collective-permute-start | bytes 153608 | tf_op jit(solution)/shard_map/ppermute | solution.py:36
  30.4 0.4 collective-permute-done.8.refs_1_.b_second
  30.9 1.9 %shard_map.86 = bf16[3,8,3360]{2,1,0:T(8,128)(2,1)S(1)} custom-call(s32[5]{0:T(128)S(1)} %stack.35.info, bf16[6,2,8,3360]{3,2,1,0:T(8,128)(2,1)S(1)} %collective-permute-done.4.first, bf16[6,2,8,3360]{3,2,1,0:T(8,128)(2,1)S(1)} %collective-permute-done.5.second, bf16[3,2,8,3360]{3,2,1,0:T(8,128)(2,1)S(1)} %collective-permute-done.7.refs_0_.b_first, ...), custom_call_target="tpu_custom_call" | custom-call | tf_op jit(solution)/shard_map/pallas_call | solution.py:46
  32.7 2.0 %collective-permute-start.9 = (bf16[3,8,3360]{2,1,0:T(8,128)(2,1)S(1)}, bf16[3,8,3360]{2,1,0:T(8,128)(2,1)S(1)}, u32[]{:S(2)}, u32[]{:S(2)}) collective-permute-start(bf16[3,8,3360]{2,1,0:T(8,128)(2,1)S(1)} %shard_map.86), channel_id=1, source_target_pairs={{0,4},{4,8},{8,12},{12,0},{1,5},{5,9},{9,13},{13,1},{2,6},{6,10},{... | collective-permute-start | bytes 483848 | tf_op jit(solution)/shard_map/ppermute | solution.py:36
  34.8 5.4 %collective-permute-done.1.earlier = bf16[40,640]{1,0:T(8,128)(2,1)S(1)} collective-permute-done((bf16[40,640]{1,0:T(8,128)(2,1)S(1)}, bf16[40,640]{1,0:T(8,128)(2,1)S(1)}, u32[]{:S(2)}, u32[]{:S(2)}) %collective-permute-start.1) | collective-permute-done | bytes 51232 | tf_op jit(solution)/shard_map/ppermute | solution.py:36
  40.1 0.6 shard_map.80
  40.7 0.1 collective-permute-start.2
  40.8 5.0 %collective-permute-done.2.earlier = bf16[40,640]{1,0:T(8,128)(2,1)S(1)} collective-permute-done((bf16[40,640]{1,0:T(8,128)(2,1)S(1)}, bf16[40,640]{1,0:T(8,128)(2,1)S(1)}, u32[]{:S(2)}, u32[]{:S(2)}) %collective-permute-start.2) | collective-permute-done | bytes 51232 | tf_op jit(solution)/shard_map/ppermute | solution.py:36
  45.8 1.2 %shard_map.81 = (f32[40,640]{1,0:T(8,128)S(1)}, bf16[40,640]{1,0:T(8,128)(2,1)}) custom-call(s32[5]{0:T(128)S(1)} %stack.35.info, f32[40,640]{1,0:T(8,128)S(1)} %get-tuple-element.14.own, bf16[40,640]{1,0:T(8,128)(2,1)S(1)} %collective-permute-done.2.earlier), custom_call_target="tpu_custom_call" | custom-call | tf_op jit(solution)/shard_map/pallas_call | solution.py:46
  47.0 1.5 %collective-permute-start.3 = (f32[40,640]{1,0:T(8,128)S(1)}, f32[40,640]{1,0:T(8,128)S(1)}, u32[]{:S(2)}, u32[]{:S(2)}) collective-permute-start(f32[40,640]{1,0:T(8,128)S(1)} %get-tuple-element.16.own), channel_id=1, source_target_pairs={{0,2},{2,0},{1,3},{3,1},{4,6},{6,4},{5,7},{7,5},{8,10},{10,8},{9,1... | collective-permute-start | bytes 307208 | tf_op jit(solution)/shard_map/ppermute | solution.py:36
  48.4 3.2 %collective-permute-done.3.refs_0_ = f32[40,640]{1,0:T(8,128)S(1)} collective-permute-done((f32[40,640]{1,0:T(8,128)S(1)}, f32[40,640]{1,0:T(8,128)S(1)}, u32[]{:S(2)}, u32[]{:S(2)}) %collective-permute-start.3) | collective-permute-done | bytes 102432 | tf_op jit(solution)/shard_map/ppermute | solution.py:36
  51.6 2.0 %shard_map.82 = bf16[128,1120]{1,0:T(8,128)(2,1)} custom-call(s32[5]{0:T(128)S(1)} %stack.35.info, bf16[128,1120]{1,0:T(8,128)(2,1)S(1)} %bitcast.18, f32[40,640]{1,0:T(8,128)S(1)} %get-tuple-element.16.own, f32[40,640]{1,0:T(8,128)S(1)} %collective-permute-done.3.refs_0_), custom_call_target="tpu_custom_call" | custom-call | tf_op jit(solution)/shard_map/pallas_call | solution.py:46
  53.6 3.8 %shard_map.87.gated = bf16[2,8,8,3360]{3,2,1,0:T(8,128)(2,1)} custom-call(s32[5]{0:T(128)S(1)} %stack.35.info, bf16[6,2,8,3360]{3,2,1,0:T(8,128)(2,1)S(1)} %collective-permute-done.4.first, bf16[6,2,8,3360]{3,2,1,0:T(8,128)(2,1)S(1)} %collective-permute-done.5.second, bf16[3,2,8,3360]{3,2,1,0:T(8,128)(2,1)S(1)} %collective-permute-done.7.refs_0_.b_first, ...), custom_call_target="tpu_custom_call" | custom-call | tf_op jit(solution)/shard_map/pallas_call | solution.py:46
  57.4 0.6 %shard_map.88 = bf16[2,8,8,3360]{3,2,1,0:T(8,128)(2,1)} custom-call(s32[5]{0:T(128)S(1)} %stack.35.info, bf16[4,8,3360]{2,1,0:T(8,128)(2,1)S(1)} %collective-permute-done.6.rows, bf16[3,8,3360]{2,1,0:T(8,128)(2,1)S(1)} %collective-permute-done.9.more, bf16[2,8,8,3360]{3,2,1,0:T(8,128)(2,1)} %shard_map.87.gated), custom_call_target="tpu_custom_call", output_to_operand_aliasing={{}: (3, {})} | custom-call | tf_op jit(solution)/shard_map/pallas_call | solution.py:46
  (12 shorter events, 0.0 us)
Async XLA Ops:
  0.6 1.8 %copy-start = (f32[3,3,2,3360]{3,2,1,0:T(2,128)S(1)}, f32[3,3,2,3360]{3,2,1,0:T(2,128)}, u32[]{:S(2)}) copy-start(f32[3,3,2,3360]{3,2,1,0:T(2,128)} %refs_6_.1) | copy-start | bytes 725764
  2.4 5.0 %copy-start.2 = (bf16[2,8,8,1120]{3,2,1,0:T(8,128)(2,1)S(1)}, bf16[2,8,8,1120]{3,2,1,0:T(8,128)(2,1)}, u32[]{:S(2)}) copy-start(bf16[2,8,8,1120]{3,2,1,0:T(8,128)(2,1)} %param.7) | copy-start | bytes 860164
  2.4 5.0 %copy-start.3 = (bf16[2,8,8,1120]{3,2,1,0:T(8,128)(2,1)S(1)}, bf16[2,8,8,1120]{3,2,1,0:T(8,128)(2,1)}, u32[]{:S(2)}) copy-start(bf16[2,8,8,1120]{3,2,1,0:T(8,128)(2,1)} %param.8) | copy-start | bytes 860164
  4.3 18.8 %collective-permute-start.4 = (bf16[6,2,8,3360]{3,2,1,0:T(8,128)(2,1)S(1)}, bf16[6,2,8,3360]{3,2,1,0:T(8,128)(2,1)S(1)}, u32[]{:S(2)}, u32[]{:S(2)}) collective-permute-start(bf16[6,2,8,3360]{3,2,1,0:T(8,128)(2,1)S(1)} %get-tuple-element.17.refs_0_.refs_2_.sent_first), channel_id=1, source_target_pairs={{0,4},{4,8},{8,12},{12,28},{16,0},{20,16},{24,20},{28,24},{1,5},{5... | collective-permute-start | bytes 1935368 | tf_op jit(solution)/shard_map/ppermute | solution.py:31
  7.4 17.8 %collective-permute-start.5 = (bf16[6,2,8,3360]{3,2,1,0:T(8,128)(2,1)S(1)}, bf16[6,2,8,3360]{3,2,1,0:T(8,128)(2,1)S(1)}, u32[]{:S(2)}, u32[]{:S(2)}) collective-permute-start(bf16[6,2,8,3360]{3,2,1,0:T(8,128)(2,1)S(1)} %get-tuple-element.18.refs_1_.refs_3_.sent_second), channel_id=1, source_target_pairs={{0,16},{4,0},{8,4},{12,8},{16,20},{20,24},{24,28},{28,12},{1,17},{... | collective-permute-start | bytes 1935368 | tf_op jit(solution)/shard_map/ppermute | solution.py:31
  8.3 8.1 %collective-permute-start = (bf16[5,8,3360]{2,1,0:T(8,128)(2,1)S(1)}, bf16[5,8,3360]{2,1,0:T(8,128)(2,1)S(1)}, u32[]{:S(2)}, u32[]{:S(2)}) collective-permute-start(bf16[5,8,3360]{2,1,0:T(8,128)(2,1)S(1)} %shard_map.78), channel_id=1, source_target_pairs={{0,2},{2,0},{1,3},{3,1},{4,6},{6,4},{5,7},{7,5},{8,10},{10,8},{9,1... | collective-permute-start | bytes 806408 | tf_op jit(solution)/shard_map/ppermute | solution.py:36
  18.0 7.2 %copy-start.1 = (f32[3,2,3360]{2,1,0:T(2,128)S(1)}, f32[3,2,3360]{2,1,0:T(2,128)}, u32[]{:S(2)}) copy-start(f32[3,2,3360]{2,1,0:T(2,128)} %temporal.1) | copy-start | bytes 241924
  18.0 12.5 %collective-permute-start.7 = (bf16[3,2,8,3360]{3,2,1,0:T(8,128)(2,1)S(1)}, bf16[3,2,8,3360]{3,2,1,0:T(8,128)(2,1)S(1)}, u32[]{:S(2)}, u32[]{:S(2)}) collective-permute-start(bf16[3,2,8,3360]{3,2,1,0:T(8,128)(2,1)S(1)} %get-tuple-element.19), channel_id=1, source_target_pairs={{0,4},{4,8},{8,12},{12,28},{16,0},{20,16},{24,20},{28,24},{1,5},{5... | collective-permute-start | bytes 967688 | tf_op jit(solution)/shard_map/ppermute | solution.py:31
  19.8 11.1 %collective-permute-start.8 = (bf16[3,2,8,3360]{3,2,1,0:T(8,128)(2,1)S(1)}, bf16[3,2,8,3360]{3,2,1,0:T(8,128)(2,1)S(1)}, u32[]{:S(2)}, u32[]{:S(2)}) collective-permute-start(bf16[3,2,8,3360]{3,2,1,0:T(8,128)(2,1)S(1)} %get-tuple-element.20), channel_id=1, source_target_pairs={{0,16},{4,0},{8,4},{12,8},{16,20},{20,24},{24,28},{28,12},{1,17},{... | collective-permute-start | bytes 967688 | tf_op jit(solution)/shard_map/ppermute | solution.py:31
  27.2 30.2 %collective-permute-start.6 = (bf16[4,8,3360]{2,1,0:T(8,128)(2,1)S(1)}, bf16[4,8,3360]{2,1,0:T(8,128)(2,1)S(1)}, u32[]{:S(2)}, u32[]{:S(2)}) collective-permute-start(bf16[4,8,3360]{2,1,0:T(8,128)(2,1)S(1)} %shard_map.85), channel_id=1, source_target_pairs={{0,4},{4,8},{8,12},{12,0},{1,5},{5,9},{9,13},{13,1},{2,6},{6,10},{... | collective-permute-start | bytes 645128 | tf_op jit(solution)/shard_map/ppermute | solution.py:36
  28.9 11.3 %collective-permute-start.1 = (bf16[40,640]{1,0:T(8,128)(2,1)S(1)}, bf16[40,640]{1,0:T(8,128)(2,1)S(1)}, u32[]{:S(2)}, u32[]{:S(2)}) collective-permute-start(bf16[40,640]{1,0:T(8,128)(2,1)S(1)} %get-tuple-element.13), channel_id=1, source_target_pairs={{0,4},{4,8},{8,12},{12,0},{1,5},{5,9},{9,13},{13,1},{2,6},{6,10},{... | collective-permute-start | bytes 153608 | tf_op jit(solution)/shard_map/ppermute | solution.py:36
  30.9 20.8 %copy-start.4 = (bf16[2,8,8,1120]{3,2,1,0:T(8,128)(2,1)S(1)}, bf16[2,8,8,1120]{3,2,1,0:T(8,128)(2,1)}, u32[]{:S(2)}) copy-start(bf16[2,8,8,1120]{3,2,1,0:T(8,128)(2,1)} %param.6) | copy-start | bytes 860164
  32.7 24.7 %collective-permute-start.9 = (bf16[3,8,3360]{2,1,0:T(8,128)(2,1)S(1)}, bf16[3,8,3360]{2,1,0:T(8,128)(2,1)S(1)}, u32[]{:S(2)}, u32[]{:S(2)}) collective-permute-start(bf16[3,8,3360]{2,1,0:T(8,128)(2,1)S(1)} %shard_map.86), channel_id=1, source_target_pairs={{0,4},{4,8},{8,12},{12,0},{1,5},{5,9},{9,13},{13,1},{2,6},{6,10},{... | collective-permute-start | bytes 483848 | tf_op jit(solution)/shard_map/ppermute | solution.py:36
  40.7 5.1 %collective-permute-start.2 = (bf16[40,640]{1,0:T(8,128)(2,1)S(1)}, bf16[40,640]{1,0:T(8,128)(2,1)S(1)}, u32[]{:S(2)}, u32[]{:S(2)}) collective-permute-start(bf16[40,640]{1,0:T(8,128)(2,1)S(1)} %get-tuple-element.15), channel_id=1, source_target_pairs={{0,8},{4,12},{8,0},{12,4},{1,9},{5,13},{9,1},{13,5},{2,10},{6,14},... | collective-permute-start | bytes 153608 | tf_op jit(solution)/shard_map/ppermute | solution.py:36
  47.0 4.7 %collective-permute-start.3 = (f32[40,640]{1,0:T(8,128)S(1)}, f32[40,640]{1,0:T(8,128)S(1)}, u32[]{:S(2)}, u32[]{:S(2)}) collective-permute-start(f32[40,640]{1,0:T(8,128)S(1)} %get-tuple-element.16.own), channel_id=1, source_target_pairs={{0,2},{2,0},{1,3},{3,1},{4,6},{6,4},{5,7},{7,5},{8,10},{10,8},{9,1... | collective-permute-start | bytes 307208 | tf_op jit(solution)/shard_map/ppermute | solution.py:36
